TPU v7x, 32 devices: a whole 2x2x4 slice. The times are simulated.
32 devices in a mesh: seq: 8 (over y, x, core), ft: 4 (over z).
Axes of the slice: x: 2, y: 2, z: 4, core: 2. Of those that a mesh axis runs over, the one named last changes fastest.
Arguments:
- video: bfloat16 [8, 8, 196, 768], P('seq', None, 'ft'), may hold values from -6 to 6
- class_token: bfloat16 [8, 768], P('seq'), may hold values from -6 to 6
- frame_clip: int32 [8, 8], P('seq'), may hold values from 0 to 2, never falling along the last dimension, each value on 1 to 4 neighbouring positions
- patch_clip: int32 [8, 196], P('seq'), may hold values from 0 to 3, never falling along the last dimension, each value on 1 to 98 neighbouring positions
- padding: int32 [8, 196], P('seq'), may hold values 0 or 1
- time_gain: bfloat16 [768], P('ft'), may hold values from 0.099609375 to 1.8984375
- time_shift: bfloat16 [768], P('ft'), may hold values from -1 to 1
- time_project: bfloat16 [768, 2304], P('ft'), may hold values from -0.21875 to 0.21875
- time_output: bfloat16 [768, 768], P('ft'), may hold values from -0.3125 to 0.3125
- time_output_bias: bfloat16 [768], P('ft'), may hold values from -1 to 1
- time_mixer: bfloat16 [768, 768], P('ft'), may hold values from -0.21875 to 0.21875
- time_mixer_bias: bfloat16 [768], P('ft'), may hold values from -1 to 1
- space_gain: bfloat16 [768], P('ft'), may hold values from 0.099609375 to 1.8984375
- space_shift: bfloat16 [768], P('ft'), may hold values from -1 to 1
- space_project: bfloat16 [768, 2304], P('ft'), may hold values from -0.21875 to 0.21875
- space_output: bfloat16 [768, 768], P('ft'), may hold values from -1.25 to 1.25
- space_output_bias: bfloat16 [768], P('ft'), may hold values from -1 to 1
- feed_gain: bfloat16 [768], P('ft'), may hold values from 0.099609375 to 1.8984375
- feed_shift: bfloat16 [768], P('ft'), may hold values from -1 to 1
- feed_expand: bfloat16 [768, 3072], P('ft'), may hold values from -0.21875 to 0.21875
- feed_expand_bias: bfloat16 [3072], P('ft'), may hold values from -1 to 1
- feed_reduce: bfloat16 [3072, 768], P('ft'), may hold values from -0.109375 to 0.109375
- feed_reduce_bias: bfloat16 [768], P('ft'), may hold values from -1 to 1
- grad_output: bfloat16 [8, 8, 196, 768], P('seq', 'ft'), may hold values from -6 to 6
- grad_class_out: bfloat16 [8, 768], P('seq'), may hold values from -6 to 6
Outputs:
- output: bfloat16 [8, 8, 196, 768], P('seq', 'ft')
- class_output: bfloat16 [8, 768], P('seq')
- grad_video: float32 [8, 8, 196, 768], P('seq', None, 'ft')
- grad_class: float32 [8, 768], P('seq')
- grad_time_gain: float32 [768], P(('seq', 'ft'))
- grad_time_shift: float32 [768], P(('seq', 'ft'))
- grad_time_project: float32 [768, 2304], P(('seq', 'ft'))
- grad_time_output: float32 [768, 768], P(('seq', 'ft'))
- grad_time_output_bias: float32 [768], P(('seq', 'ft'))
- grad_time_mixer: float32 [768, 768], P(('seq', 'ft'))
- grad_time_mixer_bias: float32 [768], P(('seq', 'ft'))
- grad_space_gain: float32 [768], P(('seq', 'ft'))
- grad_space_shift: float32 [768], P(('seq', 'ft'))
- grad_space_project: float32 [768, 2304], P(('seq', 'ft'))
- grad_space_output: float32 [768, 768], P(('seq', 'ft'))
- grad_space_output_bias: float32 [768], P(('seq', 'ft'))
- grad_feed_gain: float32 [768], P(('seq', 'ft'))
- grad_feed_shift: float32 [768], P(('seq', 'ft'))
- grad_feed_expand: float32 [768, 3072], P(('seq', 'ft'))
- grad_feed_expand_bias: float32 [3072], P(('seq', 'ft'))
- grad_feed_reduce: float32 [3072, 768], P(('seq', 'ft'))
- grad_feed_reduce_bias: float32 [768], P(('seq', 'ft'))
Inputs may be any that keep to these rules, and one draw needn't show every extreme that they name: Along the 8 frames of a sequence frame_clip never falls; frames with equal values form one clip. Along the 196 patch positions patch_clip never falls. 1 marks a padding patch position.
All inputs are finite; a program needn't handle non-finite values. No bound on the sum of `padding` on one device may be relied on, other than what follows from the above.
Results may differ from a plain program's by a relative error of at most 0.025.
Values may be sent and summed in bfloat16 or wider, within the bound.
A program may use at most 256 MiB of HBM per device.

v0:
```python
from functools import partial

import jax
import jax.numpy as jnp
from jax import lax
from jax.sharding import PartitionSpec as P

HEADS = 12
HD = 64


epsilon = 1e-06


def layer_norm(values, gain, shift):
    centre = jnp.mean(values, axis=-1, keepdims=True)
    centred = values - centre
    spread = jnp.mean(centred * centred, axis=-1, keepdims=True)
    return centred * lax.rsqrt(spread + epsilon) * gain + shift


def norm_pull(values, gain, shift, cotangent):
    unused, pull = jax.vjp(layer_norm, values, gain, shift)
    return pull(cotangent)


def matmul(left, right):
    return jnp.dot(left, right, preferred_element_type=jnp.float32)


def times_transposed(left, right):
    return lax.dot_general(
        left, right, (((1,), (1,)), ((), ())), preferred_element_type=jnp.float32
    )


def transposed_times(left, right):
    return lax.dot_general(
        left, right, (((0,), (0,)), ((), ())), preferred_element_type=jnp.float32
    )


def column_sum(values):
    return jnp.sum(values, axis=0, dtype=jnp.float32)


def reorder_rows(values, outer_count, inner_count):
    rest = values.shape[1:]
    blocks = values.reshape((outer_count, inner_count, -1) + rest)
    blocks = jnp.swapaxes(blocks, 0, 1)
    return blocks.reshape(values.shape)


def row_blocks(values, count):
    return values.reshape((count, values.shape[0] // count) + values.shape[1:])


def split_heads(joined):
    shape = joined.shape[:-1]
    split = joined.reshape(shape + (3, HEADS, HD))
    return (split[..., 0, :, :], split[..., 1, :, :], split[..., 2, :, :])


def score_blocks(query, keys, allowed, form, other):
    scores = jnp.einsum(
        form + "he," + other + "he->abhlm", query, keys, preferred_element_type=jnp.float32
    ) * HD ** (-0.5)
    return jnp.where(allowed, scores, -1e30)


def attend_forward(joined, allowed, form):
    other = form.replace("l", "m")
    query, keys, values = split_heads(joined)
    scores = score_blocks(query, keys, allowed, form, other)
    row_top = jnp.max(scores, axis=-1, keepdims=True)
    exponent = jnp.exp(scores - row_top)
    row_total = jnp.sum(exponent, axis=-1, keepdims=True)
    probability = (exponent / row_total).astype(jnp.bfloat16)
    mixed = jnp.einsum(
        "abhlm," + other + "he->" + form + "he",
        probability,
        values,
        preferred_element_type=jnp.float32,
    )
    return (
        mixed.reshape(joined.shape[:-1] + (HEADS * HD,)).astype(jnp.bfloat16),
        row_top + jnp.log(row_total),
    )


def attend_backward(joined, allowed, log_total, grad_mixed, form):
    other = form.replace("l", "m")
    query, keys, values = split_heads(joined)
    scores = score_blocks(query, keys, allowed, form, other)
    probability = jnp.exp(scores - log_total)
    grad_heads = grad_mixed.reshape(query.shape)
    grad_prob = jnp.einsum(
        form + "he," + other + "he->abhlm", grad_heads, values, preferred_element_type=jnp.float32
    )
    grad_values = jnp.einsum(
        "abhlm," + form + "he->" + other + "he",
        probability.astype(jnp.bfloat16),
        grad_heads,
        preferred_element_type=jnp.float32,
    )
    inner = jnp.sum(probability * grad_prob, axis=-1, keepdims=True)
    grad_scores = (probability * (grad_prob - inner)).astype(jnp.bfloat16)
    grad_query = jnp.einsum(
        "abhlm," + other + "he->" + form + "he",
        grad_scores,
        keys,
        preferred_element_type=jnp.float32,
    ) * HD ** (-0.5)
    grad_keys = jnp.einsum(
        "abhlm," + form + "he->" + other + "he",
        grad_scores,
        query,
        preferred_element_type=jnp.float32,
    ) * HD ** (-0.5)
    stacked = jnp.stack([grad_query, grad_keys, grad_values], axis=-3)
    return stacked.reshape(joined.shape).astype(jnp.bfloat16)


def shards(
    video,
    class_token,
    frame_clip,
    patch_clip,
    padding,
    time_gain,
    time_shift,
    time_project,
    time_output,
    time_output_bias,
    time_mixer,
    time_mixer_bias,
    space_gain,
    space_shift,
    space_project,
    space_output,
    space_output_bias,
    feed_gain,
    feed_shift,
    feed_expand,
    feed_expand_bias,
    feed_reduce,
    feed_reduce_bias,
    grad_output,
    grad_class_out,
):
    (
        time_gain,
        time_shift,
        time_project,
        time_output,
        time_output_bias,
        time_mixer,
        time_mixer_bias,
        space_gain,
        space_shift,
        space_project,
        space_output,
        space_output_bias,
        feed_gain,
        feed_shift,
        feed_expand,
        feed_expand_bias,
        feed_reduce,
        feed_reduce_bias,
    ) = (
        lax.all_gather(time_gain, "ft", axis=0, tiled=True),
        lax.all_gather(time_shift, "ft", axis=0, tiled=True),
        lax.all_gather(time_project, "ft", axis=0, tiled=True),
        lax.all_gather(time_output, "ft", axis=0, tiled=True),
        lax.all_gather(time_output_bias, "ft", axis=0, tiled=True),
        lax.all_gather(time_mixer, "ft", axis=0, tiled=True),
        lax.all_gather(time_mixer_bias, "ft", axis=0, tiled=True),
        lax.all_gather(space_gain, "ft", axis=0, tiled=True),
        lax.all_gather(space_shift, "ft", axis=0, tiled=True),
        lax.all_gather(space_project, "ft", axis=0, tiled=True),
        lax.all_gather(space_output, "ft", axis=0, tiled=True),
        lax.all_gather(space_output_bias, "ft", axis=0, tiled=True),
        lax.all_gather(feed_gain, "ft", axis=0, tiled=True),
        lax.all_gather(feed_shift, "ft", axis=0, tiled=True),
        lax.all_gather(feed_expand, "ft", axis=0, tiled=True),
        lax.all_gather(feed_expand_bias, "ft", axis=0, tiled=True),
        lax.all_gather(feed_reduce, "ft", axis=0, tiled=True),
        lax.all_gather(feed_reduce_bias, "ft", axis=0, tiled=True),
    )
    time_gain = time_gain.astype(jnp.float32)
    time_shift = time_shift.astype(jnp.float32)
    space_gain = space_gain.astype(jnp.float32)
    space_shift = space_shift.astype(jnp.float32)
    feed_gain = feed_gain.astype(jnp.float32)
    feed_shift = feed_shift.astype(jnp.float32)
    time_output_bias = time_output_bias.astype(jnp.float32)
    time_mixer_bias = time_mixer_bias.astype(jnp.float32)
    space_output_bias = space_output_bias.astype(jnp.float32)
    feed_expand_bias = feed_expand_bias.astype(jnp.float32)
    feed_reduce_bias = feed_reduce_bias.astype(jnp.float32)
    seqs_here, frames, patch_here, width = video.shape
    frames_here = frames // lax.axis_size("ft")
    patches = patch_clip.shape[1]
    length = patches + 1
    total_rows = seqs_here * frames * patch_here
    patch_count = seqs_here * frames_here * patches
    time_rows = video.astype(jnp.float32).reshape(total_rows, width)
    time_normed = layer_norm(time_rows, time_gain, time_shift).astype(jnp.bfloat16)
    time_joined = (
        matmul(time_normed, time_project)
        .astype(jnp.bfloat16)
        .reshape(seqs_here, frames, patch_here, 3 * width)
    )
    same_clip = frame_clip[:, :, None] == frame_clip[:, None, :]
    time_allowed = same_clip[:, None, None, :, :]
    time_mixed, time_total = attend_forward(time_joined, time_allowed, "alb")
    time_outer = (
        matmul(time_mixed.reshape(total_rows, width), time_output) + time_output_bias
    ).astype(jnp.bfloat16)
    time_branch = matmul(time_outer, time_mixer) + time_mixer_bias
    after_time = (
        (time_rows + time_branch).astype(jnp.bfloat16).reshape(seqs_here, frames, patch_here, width)
    )
    after_space = lax.all_to_all(after_time, "ft", split_axis=1, concat_axis=2, tiled=True)
    class_rows = class_token.astype(jnp.float32)
    space_rows = jnp.concatenate(
        [
            jnp.broadcast_to(class_rows[:, None, None, :], (seqs_here, frames_here, 1, width)),
            after_space.astype(jnp.float32),
        ],
        axis=2,
    )
    space_normed = layer_norm(space_rows, space_gain, space_shift).astype(jnp.bfloat16)
    space_joined = (
        matmul(space_normed.reshape(-1, width), space_project)
        .astype(jnp.bfloat16)
        .reshape(seqs_here, frames_here, length, 3 * width)
    )
    key_open = jnp.concatenate([jnp.ones((seqs_here, 1), jnp.bool_), padding == 0], axis=1)
    group_ids = jnp.concatenate([jnp.full((seqs_here, 1), -1, jnp.int32), patch_clip], axis=1)
    position = jnp.arange(length)
    from_class = position == 0
    space_allowed = key_open[:, None, :] & (
        (group_ids[:, :, None] == group_ids[:, None, :])
        | from_class[None, :, None]
        | from_class[None, None, :]
    )
    space_allowed = space_allowed[:, None, None, :, :]
    space_mixed, space_total = attend_forward(space_joined, space_allowed, "abl")
    space_branch = (
        matmul(space_mixed.reshape(-1, width), space_output) + space_output_bias
    ).reshape(seqs_here, frames_here, length, width)
    class_sum = lax.psum(jnp.sum(space_branch[:, :, 0], axis=1), "ft")
    class_mid = class_rows + class_sum / frames
    patch_mid = after_space.astype(jnp.float32) + space_branch[:, :, 1:]
    feed_rows = jnp.concatenate([patch_mid.reshape(patch_count, width), class_mid], axis=0)
    feed_normed = layer_norm(feed_rows, feed_gain, feed_shift).astype(jnp.bfloat16)
    hidden = matmul(feed_normed, feed_expand) + feed_expand_bias
    active = jax.nn.gelu(hidden, approximate=False).astype(jnp.bfloat16)
    result = feed_rows + matmul(active, feed_reduce) + feed_reduce_bias
    output = (
        result[:patch_count].reshape(seqs_here, frames_here, patches, width).astype(jnp.bfloat16)
    )
    class_output = result[patch_count:].astype(jnp.bfloat16)
    first = (lax.axis_index("ft") == 0).astype(jnp.bfloat16)
    first_wide = first.astype(jnp.float32)
    grad_patch_rows = grad_output.reshape(patch_count, width)
    grad_result = jnp.concatenate([grad_patch_rows, grad_class_out], axis=0)
    grad_counted = jnp.concatenate([grad_patch_rows, grad_class_out * first], axis=0)
    grad_feed_reduce = transposed_times(active, grad_counted)
    grad_feed_reduce_bias = column_sum(grad_counted)
    grad_active = times_transposed(grad_result, feed_reduce)
    unused, gelu_pull = jax.vjp(partial(jax.nn.gelu, approximate=False), hidden)
    grad_hidden = gelu_pull(grad_active)[0].astype(jnp.bfloat16)
    hidden_counted = jnp.concatenate(
        [grad_hidden[:patch_count], grad_hidden[patch_count:] * first], axis=0
    )
    grad_feed_expand = transposed_times(feed_normed, hidden_counted)
    grad_feed_expand_bias = column_sum(hidden_counted)
    grad_feed_normed = times_transposed(grad_hidden, feed_expand)
    patch_grad, gain_patch, shift_patch = norm_pull(
        feed_rows[:patch_count], feed_gain, feed_shift, grad_feed_normed[:patch_count]
    )
    class_grad, gain_class, shift_class = norm_pull(
        feed_rows[patch_count:], feed_gain, feed_shift, grad_feed_normed[patch_count:]
    )
    grad_feed_gain = gain_patch + first_wide * gain_class
    grad_feed_shift = shift_patch + first_wide * shift_class
    grad_patch_mid = grad_patch_rows.astype(jnp.float32) + patch_grad
    grad_class_mid = grad_class_out.astype(jnp.float32) + class_grad
    grad_branch = jnp.concatenate(
        [
            jnp.broadcast_to(
                (grad_class_mid / frames)[:, None, None, :], (seqs_here, frames_here, 1, width)
            ),
            grad_patch_mid.reshape(seqs_here, frames_here, patches, width),
        ],
        axis=2,
    ).astype(jnp.bfloat16)
    grad_branch_rows = grad_branch.reshape(-1, width)
    grad_space_output = transposed_times(space_mixed.reshape(-1, width), grad_branch_rows)
    grad_space_output_bias = column_sum(grad_branch_rows)
    grad_space_mixed = times_transposed(grad_branch_rows, space_output).astype(jnp.bfloat16)
    grad_space_joined = attend_backward(
        space_joined, space_allowed, space_total, grad_space_mixed, "abl"
    ).reshape(-1, 3 * width)
    grad_space_project = transposed_times(space_normed.reshape(-1, width), grad_space_joined)
    grad_space_normed = times_transposed(grad_space_joined, space_project).reshape(
        seqs_here, frames_here, length, width
    )
    grad_space_rows, grad_space_gain, grad_space_shift = norm_pull(
        space_rows, space_gain, space_shift, grad_space_normed
    )
    class_frames = lax.psum(jnp.sum(grad_space_rows[:, :, 0], axis=1), "ft")
    grad_class = grad_class_mid + class_frames
    grad_after_space = (
        grad_patch_mid.reshape(seqs_here, frames_here, patches, width) + grad_space_rows[:, :, 1:]
    ).astype(jnp.bfloat16)
    grad_after_time = lax.all_to_all(
        grad_after_space, "ft", split_axis=2, concat_axis=1, tiled=True
    )
    grad_time_branch = grad_after_time.reshape(total_rows, width)
    grad_time_mixer = transposed_times(time_outer, grad_time_branch)
    grad_time_mixer_bias = column_sum(grad_time_branch)
    grad_time_outer = times_transposed(grad_time_branch, time_mixer).astype(jnp.bfloat16)
    grad_time_output = transposed_times(time_mixed.reshape(total_rows, width), grad_time_outer)
    grad_time_output_bias = column_sum(grad_time_outer)
    grad_time_mixed = times_transposed(grad_time_outer, time_output).astype(jnp.bfloat16)
    grad_time_joined = attend_backward(
        time_joined, time_allowed, time_total, grad_time_mixed, "alb"
    ).reshape(total_rows, 3 * width)
    grad_time_project = transposed_times(time_normed, grad_time_joined)
    grad_time_normed = times_transposed(grad_time_joined, time_project)
    grad_time_rows, grad_time_gain, grad_time_shift = norm_pull(
        time_rows, time_gain, time_shift, grad_time_normed
    )
    grad_video = (grad_time_branch.astype(jnp.float32) + grad_time_rows).reshape(
        seqs_here, frames, patch_here, width
    )
    local = (
        grad_time_gain,
        grad_time_shift,
        grad_time_project,
        grad_time_output,
        grad_time_output_bias,
        grad_time_mixer,
        grad_time_mixer_bias,
        grad_space_gain,
        grad_space_shift,
        grad_space_project,
        grad_space_output,
        grad_space_output_bias,
        grad_feed_gain,
        grad_feed_shift,
        grad_feed_expand,
        grad_feed_expand_bias,
        grad_feed_reduce,
        grad_feed_reduce_bias,
    )
    seq_count = lax.axis_size("seq")
    ft_count = lax.axis_size("ft")
    blocks = tuple(
        (row_blocks(reorder_rows(item, seq_count, ft_count), ft_count) for item in local)
    )
    moved = (
        lax.all_to_all(
            blocks[0].astype(jnp.bfloat16), "ft", split_axis=0, concat_axis=0, tiled=True
        ).astype(jnp.float32),
        lax.all_to_all(
            blocks[1].astype(jnp.bfloat16), "ft", split_axis=0, concat_axis=0, tiled=True
        ).astype(jnp.float32),
        lax.all_to_all(
            blocks[2].astype(jnp.bfloat16), "ft", split_axis=0, concat_axis=0, tiled=True
        ).astype(jnp.float32),
        lax.all_to_all(
            blocks[3].astype(jnp.bfloat16), "ft", split_axis=0, concat_axis=0, tiled=True
        ).astype(jnp.float32),
        lax.all_to_all(
            blocks[4].astype(jnp.bfloat16), "ft", split_axis=0, concat_axis=0, tiled=True
        ).astype(jnp.float32),
        lax.all_to_all(
            blocks[5].astype(jnp.bfloat16), "ft", split_axis=0, concat_axis=0, tiled=True
        ).astype(jnp.float32),
        lax.all_to_all(
            blocks[6].astype(jnp.bfloat16), "ft", split_axis=0, concat_axis=0, tiled=True
        ).astype(jnp.float32),
        lax.all_to_all(
            blocks[7].astype(jnp.bfloat16), "ft", split_axis=0, concat_axis=0, tiled=True
        ).astype(jnp.float32),
        lax.all_to_all(
            blocks[8].astype(jnp.bfloat16), "ft", split_axis=0, concat_axis=0, tiled=True
        ).astype(jnp.float32),
        lax.all_to_all(
            blocks[9].astype(jnp.bfloat16), "ft", split_axis=0, concat_axis=0, tiled=True
        ).astype(jnp.float32),
        lax.all_to_all(
            blocks[10].astype(jnp.bfloat16), "ft", split_axis=0, concat_axis=0, tiled=True
        ).astype(jnp.float32),
        lax.all_to_all(
            blocks[11].astype(jnp.bfloat16), "ft", split_axis=0, concat_axis=0, tiled=True
        ).astype(jnp.float32),
        lax.all_to_all(
            blocks[12].astype(jnp.bfloat16), "ft", split_axis=0, concat_axis=0, tiled=True
        ).astype(jnp.float32),
        lax.all_to_all(
            blocks[13].astype(jnp.bfloat16), "ft", split_axis=0, concat_axis=0, tiled=True
        ).astype(jnp.float32),
        lax.all_to_all(
            blocks[14].astype(jnp.bfloat16), "ft", split_axis=0, concat_axis=0, tiled=True
        ).astype(jnp.float32),
        lax.all_to_all(
            blocks[15].astype(jnp.bfloat16), "ft", split_axis=0, concat_axis=0, tiled=True
        ).astype(jnp.float32),
        lax.all_to_all(
            blocks[16].astype(jnp.bfloat16), "ft", split_axis=0, concat_axis=0, tiled=True
        ).astype(jnp.float32),
        lax.all_to_all(
            blocks[17].astype(jnp.bfloat16), "ft", split_axis=0, concat_axis=0, tiled=True
        ).astype(jnp.float32),
    )
    summed = tuple((jnp.sum(item, axis=0) for item in moved))
    shares = (
        lax.psum_scatter(summed[0], "seq", scatter_dimension=0, tiled=True),
        lax.psum_scatter(summed[1], "seq", scatter_dimension=0, tiled=True),
        lax.psum_scatter(summed[2], "seq", scatter_dimension=0, tiled=True),
        lax.psum_scatter(summed[3], "seq", scatter_dimension=0, tiled=True),
        lax.psum_scatter(summed[4], "seq", scatter_dimension=0, tiled=True),
        lax.psum_scatter(summed[5], "seq", scatter_dimension=0, tiled=True),
        lax.psum_scatter(summed[6], "seq", scatter_dimension=0, tiled=True),
        lax.psum_scatter(summed[7], "seq", scatter_dimension=0, tiled=True),
        lax.psum_scatter(summed[8], "seq", scatter_dimension=0, tiled=True),
        lax.psum_scatter(summed[9], "seq", scatter_dimension=0, tiled=True),
        lax.psum_scatter(summed[10], "seq", scatter_dimension=0, tiled=True),
        lax.psum_scatter(summed[11], "seq", scatter_dimension=0, tiled=True),
        lax.psum_scatter(summed[12], "seq", scatter_dimension=0, tiled=True),
        lax.psum_scatter(summed[13], "seq", scatter_dimension=0, tiled=True),
        lax.psum_scatter(summed[14], "seq", scatter_dimension=0, tiled=True),
        lax.psum_scatter(summed[15], "seq", scatter_dimension=0, tiled=True),
        lax.psum_scatter(summed[16], "seq", scatter_dimension=0, tiled=True),
        lax.psum_scatter(summed[17], "seq", scatter_dimension=0, tiled=True),
    )
    return (output, class_output, grad_video, grad_class) + tuple(shares)


def solution(mesh):
    in_specs = (
        P("seq", None, "ft", None),
        P("seq", None),
        P("seq", None),
        P("seq", None),
        P("seq", None),
        P("ft"),
        P("ft"),
        P("ft", None),
        P("ft", None),
        P("ft"),
        P("ft", None),
        P("ft"),
        P("ft"),
        P("ft"),
        P("ft", None),
        P("ft", None),
        P("ft"),
        P("ft"),
        P("ft"),
        P("ft", None),
        P("ft"),
        P("ft", None),
        P("ft"),
        P("seq", "ft", None, None),
        P("seq", None),
    )
    out_specs = (
        P("seq", "ft", None, None),
        P("seq", None),
        P("seq", None, "ft", None),
        P("seq", None),
        P(("seq", "ft")),
        P(("seq", "ft")),
        P(("seq", "ft"), None),
        P(("seq", "ft"), None),
        P(("seq", "ft")),
        P(("seq", "ft"), None),
        P(("seq", "ft")),
        P(("seq", "ft")),
        P(("seq", "ft")),
        P(("seq", "ft"), None),
        P(("seq", "ft"), None),
        P(("seq", "ft")),
        P(("seq", "ft")),
        P(("seq", "ft")),
        P(("seq", "ft"), None),
        P(("seq", "ft")),
        P(("seq", "ft"), None),
        P(("seq", "ft")),
    )
    return jax.shard_map(shards, mesh=mesh, in_specs=in_specs, out_specs=out_specs, check_vma=False)
```

profile of v0, /device:TPU:0, one launch (start us, length us, event | category | flops | bytes accessed | tf_op | source)
XLA Modules:
  0.0 1180.6 jit_solution(3627723269268127601)
XLA Ops:
  15.5 22.7 %all-reduce.22 = (bf16[768]{0:T(1024)(128)(2,1)S(1)}, bf16[768]{0:T(1024)(128)(2,1)S(1)}, bf16[768]{0:T(1024)(128)(2,1)S(1)}, bf16[768]{0:T(1024)(128)(2,1)S(1)}...) all-reduce(bf16[768]{0:T(1024)(128)(2,1)S(1)} %dynamic-update-slice, ...), channel_id=1, replica_groups=mesh['seq'=8,'ft'=4] {'ft'}, use_global_device_ids=true, to_apply=%add.8 | all-reduce | flops 7680 | bytes 30720
  39.6 43.3 %all-gather.9.cloned.1.call-done = bf16[768,2304]{1,0:T(8,128)(2,1)} async-done(((bf16[192,2304]{1,0:T(8,128)(2,1)}), bf16[768,2304]{1,0:T(8,128)(2,1)}) %all-gather.9.cloned.1.call-update) | async-done | bytes 3538960 | tf_op jit(solution)/shard_map/all_gather | solution.py:173
  105.4 8.3 all-gather.11.cloned.1.call-done
  116.4 28.4 %all-gather.13.cloned.1.call-done = bf16[768,768]{1,0:T(8,128)(2,1)} async-done(((bf16[192,768]{1,0:T(8,128)(2,1)}), bf16[768,768]{1,0:T(8,128)(2,1)}) %all-gather.13.cloned.1.call-update) | async-done | bytes 1179664 | tf_op jit(solution)/shard_map/all_gather | solution.py:176
  152.9 41.3 %all-gather = bf16[4,1,768]{2,1,0:T(2,128)(2,1)S(1)} all-gather(bf16[1,1,768]{2,1,0:T(2,128)(2,1)S(1)} %reshape.1233), channel_id=1, replica_groups=mesh['seq'=8,'ft'=4] {'ft'}, dimensions={0}, use_global_device_ids=true | all-gather | bytes 7680 | tf_op jit(solution)/shard_map/all_gather | solution.py:186
  208.0 19.4 %all-gather.15.cloned.1.call-done = bf16[768,2304]{1,0:T(8,128)(2,1)} async-done(((bf16[192,2304]{1,0:T(8,128)(2,1)}), bf16[768,2304]{1,0:T(8,128)(2,1)}) %all-gather.15.cloned.1.call-update) | async-done | bytes 3538960 | tf_op jit(solution)/shard_map/all_gather | solution.py:180
  232.7 6.6 reshape.1275
  272.8 10.3 psum.14
  297.5 51.0 %all-gather.19.cloned.1.call-done = bf16[768,3072]{1,0:T(8,128)(2,1)} async-done(((bf16[192,3072]{1,0:T(8,128)(2,1)}), bf16[768,3072]{1,0:T(8,128)(2,1)}) %all-gather.19.cloned.1.call-update) | async-done | bytes 4718608 | tf_op jit(solution)/shard_map/all_gather | solution.py:185
  348.5 16.8 %multiply_convert_fusion.1 = (bf16[393,3072]{1,0:T(8,128)(2,1)}, f32[393,3072]{1,0:T(8,128)}, f32[393,3072]{1,0:T(8,128)}) fusion(f32[3072]{0:T(1024)S(1)} %bitcast.238, bf16[768,3072]{1,0:T(8,128)(2,1)} %all-gather.19.cloned.1.call-done, f32[768]{0:T(1024)S(1)} %convert_element_type.638, f32[768]{0:T(1024)S(1)} %convert_element_type.637, ...), kind=kOutput, calls=%fused_computation.15 | convolution fusion | flops 1935899136 | bytes 18020424 | tf_op jit(solution)/shard_map/dot_general | solution.py:28
  365.3 72.7 %all-gather.21.cloned.1.call-done = bf16[3072,768]{1,0:T(8,128)(2,1)} async-done(((bf16[768,768]{1,0:T(8,128)(2,1)}), bf16[3072,768]{1,0:T(8,128)(2,1)}) %all-gather.21.cloned.1.call-update) | async-done | bytes 4718608 | tf_op jit(solution)/shard_map/all_gather | solution.py:187
  438.0 7.9 add_convert_fusion
  518.0 12.4 %all-to-all-done.1 = bf16[1,2,196,768]{3,1,0,2:T(2,128)(2,1)} async-done(((bf16[1,2,196,768]{3,1,0,2:T(2,128)(2,1)}), bf16[1,2,196,768]{3,1,0,2:T(2,128)(2,1)}, u32[]{:S(2)}, u32[]{:S(2)}) %all-to-all-start.1) | async-done | bytes 602144 | tf_op jit(solution)/shard_map/all_to_all | solution.py:319
  541.2 21.6 %all-to-all-done.12 = bf16[4,192,768]{2,1,0:T(8,128)(2,1)} async-done(((bf16[4,192,768]{2,1,0:T(8,128)(2,1)}), bf16[4,192,768]{2,1,0:T(8,128)(2,1)}, u32[]{:S(2)}, u32[]{:S(2)}) %all-to-all-start.12) | async-done | bytes 1179680 | tf_op jit(solution)/shard_map/all_to_all | solution.py:396
  575.3 19.9 %all-to-all-done.7 = bf16[4,192,768]{2,1,0:T(8,128)(2,1)} async-done(((bf16[4,192,768]{2,1,0:T(8,128)(2,1)}), bf16[4,192,768]{2,1,0:T(8,128)(2,1)}, u32[]{:S(2)}, u32[]{:S(2)}) %all-to-all-start.7) | async-done | bytes 1179680 | tf_op jit(solution)/shard_map/all_to_all | solution.py:381
  606.6 21.0 %all-to-all-done.5 = bf16[4,192,768]{2,1,0:T(8,128)(2,1)} async-done(((bf16[4,192,768]{2,1,0:T(8,128)(2,1)}), bf16[4,192,768]{2,1,0:T(8,128)(2,1)}, u32[]{:S(2)}, u32[]{:S(2)}) %all-to-all-start.5) | async-done | bytes 1179680 | tf_op jit(solution)/shard_map/all_to_all | solution.py:375
  650.2 7.0 reshape.1256
  657.2 6.6 convert_element_type.661
  674.1 37.2 %all-to-all-done.11 = bf16[4,192,2304]{2,1,0:T(8,128)(2,1)} async-done(((bf16[4,192,2304]{2,1,0:T(8,128)(2,1)}), bf16[4,192,2304]{2,1,0:T(8,128)(2,1)}, u32[]{:S(2)}, u32[]{:S(2)}) %all-to-all-start.11) | async-done | bytes 3538976 | tf_op jit(solution)/shard_map/all_to_all | solution.py:393
  725.0 69.7 %all-to-all-done.4 = bf16[4,192,2304]{2,1,0:T(8,128)(2,1)} async-done(((bf16[4,192,2304]{2,1,0:T(8,128)(2,1)}), bf16[4,192,2304]{2,1,0:T(8,128)(2,1)}, u32[]{:S(2)}, u32[]{:S(2)}) %all-to-all-start.4) | async-done | bytes 3538976 | tf_op jit(solution)/shard_map/all_to_all | solution.py:372
  818.8 84.8 %all-to-all-done.16 = bf16[4,192,3072]{2,1,0:T(8,128)(2,1)} async-done(((bf16[4,192,3072]{2,1,0:T(8,128)(2,1)}), bf16[4,192,3072]{2,1,0:T(8,128)(2,1)}, u32[]{:S(2)}, u32[]{:S(2)}) %all-to-all-start.16) | async-done | bytes 4718624 | tf_op jit(solution)/shard_map/all_to_all | solution.py:408
  917.7 94.8 %all-to-all-done.18 = bf16[4,768,768]{2,1,0:T(8,128)(2,1)} async-done(((bf16[4,768,768]{2,1,0:T(8,128)(2,1)}), bf16[4,768,768]{2,1,0:T(8,128)(2,1)}, u32[]{:S(2)}, u32[]{:S(2)}) %all-to-all-start.18) | async-done | bytes 4718624 | tf_op jit(solution)/shard_map/all_to_all | solution.py:414
  1033.8 12.2 %psum.15 = f32[1,768]{1,0:T(1,128)S(1)} all-reduce(f32[1,768]{1,0:T(1,128)S(1)} %reduce_sum.618), channel_id=1, replica_groups=mesh['seq'=8,'ft'=4] {'ft'}, use_global_device_ids=true, to_apply=%region_27.28 | all-reduce | flops 768 | bytes 6144 | tf_op jit(solution)/shard_map/psum | solution.py:314
  1145.1 22.3 %all-reduce.21 = (f32[192]{0:T(256)S(1)}, f32[192]{0:T(256)S(1)}, f32[192]{0:T(256)S(1)}, f32[192]{0:T(256)S(1)}, f32[192]{0:T(256)S(1)}, /*index=5*/f32[192]{0:...) all-reduce(f32[192]{0:T(256)S(1)} %convert_reduce_fusion.18, ...), channel_id=2, replica_groups=mesh['seq'=8,'ft'=4] {'seq'}, use_global_device_ids=true, to_apply=%region_30.31.clone | all-reduce | flops 2688 | bytes 21504
  (487 shorter events, 422.3 us)
Async XLA Ops:
  7.2 75.7 %all-gather.9.cloned.1.call-start = ((), (), s32[]{:S(2)}) async-start(), calls=%async_computation.27 | async-start | bytes 4423680 | tf_op jit(solution)/shard_map/all_gather | solution.py:173
  7.9 105.7 %all-gather.11.cloned.1.call-start = ((), (), s32[]{:S(2)}) async-start(), calls=%async_computation.28 | async-start | bytes 1474560 | tf_op jit(solution)/shard_map/all_gather | solution.py:174
  8.7 136.2 %all-gather.13.cloned.1.call-start = ((), (), s32[]{:S(2)}) async-start(), calls=%async_computation.29 | async-start | bytes 1474560 | tf_op jit(solution)/shard_map/all_gather | solution.py:176
  9.4 218.0 %all-gather.15.cloned.1.call-start = ((), (), s32[]{:S(2)}) async-start(), calls=%async_computation.30 | async-start | bytes 4423680 | tf_op jit(solution)/shard_map/all_gather | solution.py:180
  10.0 253.8 %all-gather.17.cloned.1.call-start = ((), (), s32[]{:S(2)}) async-start(), calls=%async_computation.31 | async-start | bytes 1474560 | tf_op jit(solution)/shard_map/all_gather | solution.py:181
  10.6 337.9 %all-gather.19.cloned.1.call-start = ((), (), s32[]{:S(2)}) async-start(), calls=%async_computation.32 | async-start | bytes 5898240 | tf_op jit(solution)/shard_map/all_gather | solution.py:185
  148.4 50.2 %all-to-all-start = ((bf16[1,8,49,768]{3,2,0,1:T(8,128)(2,1)}), bf16[1,8,49,768]{3,2,0,1:T(8,128)(2,1)S(1)}, u32[]{:S(2)}, u32[]{:S(2)}) async-start(bf16[1,8,49,768]{3,2,0,1:T(8,128)(2,1)} %bitcast.7), calls=%async_computation | async-start | bytes 1376256 | tf_op jit(solution)/shard_map/all_to_all | solution.py:224
  152.0 285.9 %all-gather.21.cloned.1.call-start = ((), (), s32[]{:S(2)}) async-start(), calls=%async_computation.33 | async-start | bytes 5898240 | tf_op jit(solution)/shard_map/all_gather | solution.py:187
  509.7 20.7 %all-to-all-start.1 = ((bf16[1,2,196,768]{3,1,0,2:T(2,128)(2,1)}), bf16[1,2,196,768]{3,1,0,2:T(2,128)(2,1)}, u32[]{:S(2)}, u32[]{:S(2)}) async-start(bf16[1,2,196,768]{3,1,0,2:T(2,128)(2,1)} %fusion.63), calls=%async_computation.1 | async-start | bytes 1204224 | tf_op jit(solution)/shard_map/all_to_all | solution.py:319
  530.4 32.4 %all-to-all-start.12 = ((bf16[4,192,768]{2,1,0:T(8,128)(2,1)}), bf16[4,192,768]{2,1,0:T(8,128)(2,1)}, u32[]{:S(2)}, u32[]{:S(2)}) async-start(bf16[4,192,768]{2,1,0:T(8,128)(2,1)} %bitcast.219), calls=%async_computation.16 | async-start | bytes 2359296 | tf_op jit(solution)/shard_map/all_to_all | solution.py:396
  562.8 32.4 %all-to-all-start.7 = ((bf16[4,192,768]{2,1,0:T(8,128)(2,1)}), bf16[4,192,768]{2,1,0:T(8,128)(2,1)}, u32[]{:S(2)}, u32[]{:S(2)}) async-start(bf16[4,192,768]{2,1,0:T(8,128)(2,1)} %bitcast.218), calls=%async_computation.9 | async-start | bytes 2359296 | tf_op jit(solution)/shard_map/all_to_all | solution.py:381
  595.2 32.4 %all-to-all-start.5 = ((bf16[4,192,768]{2,1,0:T(8,128)(2,1)}), bf16[4,192,768]{2,1,0:T(8,128)(2,1)}, u32[]{:S(2)}, u32[]{:S(2)}) async-start(bf16[4,192,768]{2,1,0:T(8,128)(2,1)} %bitcast.220), calls=%async_computation.6 | async-start | bytes 2359296 | tf_op jit(solution)/shard_map/all_to_all | solution.py:375
  627.6 83.7 %all-to-all-start.11 = ((bf16[4,192,2304]{2,1,0:T(8,128)(2,1)}), bf16[4,192,2304]{2,1,0:T(8,128)(2,1)}, u32[]{:S(2)}, u32[]{:S(2)}) async-start(bf16[4,192,2304]{2,1,0:T(8,128)(2,1)} %bitcast.213), calls=%async_computation.14 | async-start | bytes 7077888 | tf_op jit(solution)/shard_map/all_to_all | solution.py:393
  711.3 83.4 %all-to-all-start.4 = ((bf16[4,192,2304]{2,1,0:T(8,128)(2,1)}), bf16[4,192,2304]{2,1,0:T(8,128)(2,1)}, u32[]{:S(2)}, u32[]{:S(2)}) async-start(bf16[4,192,2304]{2,1,0:T(8,128)(2,1)} %bitcast.50), calls=%async_computation.4 | async-start | bytes 7077888 | tf_op jit(solution)/shard_map/all_to_all | solution.py:372
  794.7 108.9 %all-to-all-start.16 = ((bf16[4,192,3072]{2,1,0:T(8,128)(2,1)}), bf16[4,192,3072]{2,1,0:T(8,128)(2,1)}, u32[]{:S(2)}, u32[]{:S(2)}) async-start(bf16[4,192,3072]{2,1,0:T(8,128)(2,1)} %bitcast.211), calls=%async_computation.21 | async-start | bytes 9437184 | tf_op jit(solution)/shard_map/all_to_all | solution.py:408
  799.6 374.2 %reduce-scatter.16.cloned.1.call-start = ((), (), s32[]{:S(2)}) async-start(), calls=%async_computation.38 | async-start | bytes 663552 | tf_op jit(solution)/shard_map/reduce_scatter | solution.py:433
  802.0 371.8 %reduce-scatter.12.cloned.1.call-start = ((), (), s32[]{:S(2)}) async-start(), calls=%async_computation.36 | async-start | bytes 663552 | tf_op jit(solution)/shard_map/reduce_scatter | solution.py:428
  804.4 369.4 %reduce-scatter.10.cloned.1.call-start = ((), (), s32[]{:S(2)}) async-start(), calls=%async_computation.35 | async-start | bytes 663552 | tf_op jit(solution)/shard_map/reduce_scatter | solution.py:426
  806.7 367.1 %reduce-scatter.14.cloned.1.call-start = ((), (), s32[]{:S(2)}) async-start(), calls=%async_computation.37 | async-start | bytes 1990656 | tf_op jit(solution)/shard_map/reduce_scatter | solution.py:432
  903.5 108.9 %all-to-all-start.18 = ((bf16[4,768,768]{2,1,0:T(8,128)(2,1)}), bf16[4,768,768]{2,1,0:T(8,128)(2,1)}, u32[]{:S(2)}, u32[]{:S(2)}) async-start(bf16[4,768,768]{2,1,0:T(8,128)(2,1)} %bitcast.212), calls=%async_computation.24 | async-start | bytes 9437184 | tf_op jit(solution)/shard_map/all_to_all | solution.py:414
  908.5 265.3 %reduce-scatter.8.cloned.1.call-start = ((), (), s32[]{:S(2)}) async-start(), calls=%async_computation.34 | async-start | bytes 1990656 | tf_op jit(solution)/shard_map/reduce_scatter | solution.py:425
  912.7 261.1 %reduce-scatter.18.cloned.1.call-start = ((), (), s32[]{:S(2)}) async-start(), calls=%async_computation.39 | async-start | bytes 2654208 | tf_op jit(solution)/shard_map/reduce_scatter | solution.py:437
  917.7 256.2 %reduce-scatter.20.cloned.1.call-start = ((), (), s32[]{:S(2)}) async-start(), calls=%async_computation.40 | async-start | bytes 2654208 | tf_op jit(solution)/shard_map/reduce_scatter | solution.py:439
  1029.7 31.1 %all-to-all-start.14 = ((bf16[4,1,192]{2,1,0:T(2,128)(2,1)}), bf16[4,1,192]{2,1,0:T(2,128)(2,1)S(1)}, u32[]{:S(2)}, u32[]{:S(2)}) async-start(bf16[4,1,192]{2,1,0:T(2,128)(2,1)} %convert_element_type.754), calls=%async_computation.19 | async-start | bytes 8192 | tf_op jit(solution)/shard_map/all_to_all | solution.py:402
  (82 other events, 960.6 us)
Sparse Core Ops, SparseCore 0:
  9.6 73.2 all-gather.8
  84.5 29.1 all-gather.10
  115.2 29.5 all-gather.12
  146.3 81.0 all-gather.14
  228.8 29.4 all-gather.16
  259.7 88.7 all-gather.18
  350.1 87.8 all-gather.20
  804.2 35.7 reduce-scatter.15
  843.6 34.3 reduce-scatter.11
  881.6 34.3 reduce-scatter.9
  920.0 39.4 reduce-scatter.13
  963.2 39.4 reduce-scatter.7
  1006.6 42.4 reduce-scatter.17
  1053.2 42.4 reduce-scatter.19
where the time goes:
time: 1190 us; the launch traced here: 1180 us
  waiting for transfers between devices  637 us (54%)
  local copies, waits for them, and re-layouts  153 us (13%)
  matrix products  110 us (9%)
  blocking collectives  109 us (9%)
  starting transfers between devices  78.4 us (7%)
  other arithmetic  72.9 us (6%)
  between operations  20.3 us (2%)
    all_to_all x1, waiting for transfers between devices, shards(): lax.all_to_all(blocks[16].astype(jnp.bfloat16), 'ft', split_axis=0, conca...  94.8 us
    all_to_all x1, waiting for transfers between devices, shards(): lax.all_to_all(blocks[14].astype(jnp.bfloat16), 'ft', split_axis=0, conca...  84.8 us
    all_gather x1, waiting for transfers between devices, shards(): lax.all_gather(feed_reduce, 'ft', axis=0, tiled=True)  72.7 us
    all_to_all x1, waiting for transfers between devices, shards(): lax.all_to_all(blocks[2].astype(jnp.bfloat16), 'ft', split_axis=0, concat...  69.7 us
    all_gather x1, waiting for transfers between devices, shards(): lax.all_gather(feed_expand, 'ft', axis=0, tiled=True)  51 us
    unnamed x2, blocking collectives  45 us
    all_gather x1, waiting for transfers between devices, shards(): lax.all_gather(time_project, 'ft', axis=0, tiled=True)  43.3 us
    all_gather x1, blocking collectives, shards(): lax.all_gather(feed_expand_bias, 'ft', axis=0, tiled=True)  41.3 us
  transfers between devices with their start and end apart: 34, of which 23 were waited for; matrix products, arithmetic and copies ran while one was open for 22% of the time, Pallas kernels for 0%

commit v1 on v0

--- a/solution.py
+++ b/solution.py
@@ -1,8 +1,11 @@
+import functools
 from functools import partial
 
 import jax
 import jax.numpy as jnp
 from jax import lax
+from jax.experimental import pallas as pl
+from jax.experimental.pallas import tpu as pltpu
 from jax.sharding import PartitionSpec as P
 
 HEADS = 12
@@ -10,6 +13,206 @@
 
 
 epsilon = 1e-06
+
+
+MESH = pl.DeviceIdType.MESH
+
+
+def place():
+    s = lax.axis_index("seq")
+    f = lax.axis_index("ft")
+    core = lax.rem(s, 2)
+    col = lax.rem(s // 2, 2)
+    row = lax.rem(s // 4, 2)
+    return s, f, core, col, row
+
+
+def peers(s, core, col, row):
+    return (s + 1 - 2 * core, s + 2 - 4 * col, s + 4 - 8 * row)
+
+
+def greet(f, targets):
+    bar = pltpu.get_barrier_semaphore()
+    for t in targets:
+        pl.semaphore_signal(bar, inc=1, device_id=t, device_id_type=MESH)
+    pl.semaphore_wait(bar, len(targets))
+
+
+def remote(src, dst, send, recv, target):
+    return pltpu.make_async_remote_copy(
+        src_ref=src, dst_ref=dst, send_sem=send, recv_sem=recv, device_id=target, device_id_type=MESH
+    )
+
+
+def gather_kernel(count, *refs):
+    shards = refs[:count]
+    fulls = refs[count : 2 * count]
+    own, sz, rz, sx, rx, sy, ry, sc, rc, sd, rd = refs[2 * count :]
+    s, f, core, col, row = place()
+    sib, across, down = peers(s, core, col, row)
+    half = lax.rem(col + row, 2)
+    mine = 2 * half + core
+    other = 2 * (1 - half) + core
+    upper = f // 2
+    near = f + upper * (3 - 2 * f)
+    order = [upper * 3 + (1 - 2 * upper) * v for v in (1 - near, 2, 3)]
+
+    bar = pltpu.get_barrier_semaphore()
+    for t in (sib, across, down):
+        pl.semaphore_signal(bar, inc=1, device_id=(t, f), device_id_type=MESH)
+
+    @pl.when(f < 3)
+    def _():
+        pl.semaphore_signal(bar, inc=1, device_id=(s, f + 1), device_id_type=MESH)
+
+    @pl.when(f > 0)
+    def _():
+        pl.semaphore_signal(bar, inc=1, device_id=(s, f - 1), device_id_type=MESH)
+
+    @pl.when((f == 0) | (f == 3))
+    def _():
+        pl.semaphore_wait(bar, 4)
+
+    @pl.when((f > 0) & (f < 3))
+    def _():
+        pl.semaphore_wait(bar, 5)
+
+    def block(w, z, quarter):
+        rows = shards[w].shape[0]
+        part = rows // 4
+        return fulls[w].at[pl.ds(pl.multiple_of(z * rows + quarter * part, 16), part), :]
+
+    def side(w, z, quarter, which):
+        rows, wide = shards[w].shape
+        part = rows // 4
+        return fulls[w].at[
+            pl.ds(pl.multiple_of(z * rows + quarter * part, 16), part),
+            pl.ds(which * (wide // 2), wide // 2),
+        ]
+
+    def up(w, z, src):
+        return remote(src, block(w, z, mine), sz.at[w, 0, z], rz.at[w, z], (s, f + 1))
+
+    def low(w, z, src):
+        return remote(src, block(w, z, mine), sz.at[w, 1, z], rz.at[w, z], (s, f - 1))
+
+    def start_own(w):
+        rows = shards[w].shape[0]
+        part = rows // 4
+        src = shards[w].at[pl.ds(pl.multiple_of(mine * part, 16), part), :]
+
+        @pl.when(f < 3)
+        def _():
+            up(w, f, src).start()
+
+        @pl.when(f > 0)
+        def _():
+            low(w, f, src).start()
+
+        keep = pltpu.make_async_copy(
+            shards[w], fulls[w].at[pl.ds(pl.multiple_of(f * rows, 16), rows), :], own.at[w]
+        )
+        keep.start()
+
+    def to_across(w, z):
+        return remote(side(w, z, mine, 0), side(w, z, mine, 0), sx.at[w, z], rx.at[w, z], (across, f))
+
+    def to_down(w, z):
+        return remote(side(w, z, mine, 1), side(w, z, mine, 1), sy.at[w, z], ry.at[w, z], (down, f))
+
+    def to_sib(w, z):
+        return remote(block(w, z, mine), block(w, z, mine), sc.at[w, z], rc.at[w, z], (sib, f))
+
+    def to_sib_late(w, z):
+        return remote(block(w, z, other), block(w, z, other), sd.at[w, z], rd.at[w, z], (sib, f))
+
+    def relay(w):
+        for z in order:
+            low(w, z, block(w, z, mine)).wait_recv()
+
+            @pl.when((z < f) & (f < 3))
+            def _():
+                up(w, z, block(w, z, mine)).start()
+
+            @pl.when((z > f) & (f > 0))
+            def _():
+                low(w, z, block(w, z, mine)).start()
+
+            to_across(w, z).start()
+            to_down(w, z).start()
+            to_sib(w, z).start()
+
+    def late(w):
+        for z in order:
+            src = side(w, z, other, 0)
+            remote(src, src, sx.at[w, z], rx.at[w, z], (across, f)).wait_recv()
+            src = side(w, z, other, 1)
+            remote(src, src, sy.at[w, z], ry.at[w, z], (down, f)).wait_recv()
+            to_sib_late(w, z).start()
+
+    def finish(w):
+        for z in order:
+            to_sib(w, z).wait_recv()
+            to_sib_late(w, z).wait_recv()
+        rows = shards[w].shape[0]
+        pltpu.make_async_copy(
+            shards[w], fulls[w].at[pl.ds(pl.multiple_of(f * rows, 16), rows), :], own.at[w]
+        ).wait()
+
+    def drain(w):
+        for z in order:
+            to_across(w, z).wait_send()
+            to_down(w, z).wait_send()
+            to_sib(w, z).wait_send()
+            to_sib_late(w, z).wait_send()
+
+            @pl.when((z < f) & (f < 3))
+            def _():
+                up(w, z, block(w, z, mine)).wait_send()
+
+            @pl.when((z > f) & (f > 0))
+            def _():
+                low(w, z, block(w, z, mine)).wait_send()
+
+        rows = shards[w].shape[0]
+        part = rows // 4
+        src = shards[w].at[pl.ds(pl.multiple_of(mine * part, 16), part), :]
+
+        @pl.when(f < 3)
+        def _():
+            up(w, f, src).wait_send()
+
+        @pl.when(f > 0)
+        def _():
+            low(w, f, src).wait_send()
+
+    start_own(0)
+    start_own(1)
+    for w in range(count):
+        relay(w)
+        if w + 2 < count:
+            start_own(w + 2)
+        if w > 0:
+            late(w - 1)
+            finish(w - 1)
+    late(count - 1)
+    finish(count - 1)
+    for w in range(count):
+        drain(w)
+
+
+def gather(shards):
+    count = len(shards)
+    sem = pltpu.SemaphoreType.DMA
+    return pl.pallas_call(
+        functools.partial(gather_kernel, count),
+        out_shape=[jax.ShapeDtypeStruct((4 * a.shape[0], a.shape[1]), a.dtype) for a in shards],
+        in_specs=[pl.BlockSpec(memory_space=pl.ANY)] * count,
+        out_specs=[pl.BlockSpec(memory_space=pl.ANY)] * count,
+        scratch_shapes=[sem((count,)), sem((count, 2, 4))] + [sem((count, 4))] * 9,
+        compiler_params=pltpu.CompilerParams(collective_id=1, has_side_effects=True),
+        name="gather_weights",
+    )(*shards)
 
 
 def layer_norm(values, gain, shift):
@@ -148,45 +351,59 @@
     grad_output,
     grad_class_out,
 ):
+    vectors = jnp.stack(
+        [
+            time_gain,
+            time_shift,
+            time_output_bias,
+            time_mixer_bias,
+            space_gain,
+            space_shift,
+            space_output_bias,
+            feed_gain,
+            feed_shift,
+            feed_reduce_bias,
+        ]
+        + [feed_expand_bias[192 * i : 192 * (i + 1)] for i in range(4)]
+        + [jnp.zeros_like(time_gain)] * 50
+    )
+    vectors = jnp.pad(vectors, ((0, 0), (0, 64)))
+    (
+        time_project,
+        time_output,
+        time_mixer,
+        space_project,
+        space_output,
+        feed_expand,
+        feed_reduce,
+        vectors,
+    ) = gather(
+        (
+            time_project,
+            time_output,
+            time_mixer,
+            space_project,
+            space_output,
+            feed_expand,
+            feed_reduce,
+            vectors,
+        )
+    )
+    vectors = vectors.reshape(4, 64, 256)[:, :14, :192]
+    wide = jnp.swapaxes(vectors, 0, 1)[:10].reshape(10, 768)
     (
         time_gain,
         time_shift,
-        time_project,
-        time_output,
         time_output_bias,
-        time_mixer,
         time_mixer_bias,
         space_gain,
         space_shift,
-        space_project,
-        space_output,
         space_output_bias,
         feed_gain,
         feed_shift,
-        feed_expand,
-        feed_expand_bias,
-        feed_reduce,
         feed_reduce_bias,
-    ) = (
-        lax.all_gather(time_gain, "ft", axis=0, tiled=True),
-        lax.all_gather(time_shift, "ft", axis=0, tiled=True),
-        lax.all_gather(time_project, "ft", axis=0, tiled=True),
-        lax.all_gather(time_output, "ft", axis=0, tiled=True),
-        lax.all_gather(time_output_bias, "ft", axis=0, tiled=True),
-        lax.all_gather(time_mixer, "ft", axis=0, tiled=True),
-        lax.all_gather(time_mixer_bias, "ft", axis=0, tiled=True),
-        lax.all_gather(space_gain, "ft", axis=0, tiled=True),
-        lax.all_gather(space_shift, "ft", axis=0, tiled=True),
-        lax.all_gather(space_project, "ft", axis=0, tiled=True),
-        lax.all_gather(space_output, "ft", axis=0, tiled=True),
-        lax.all_gather(space_output_bias, "ft", axis=0, tiled=True),
-        lax.all_gather(feed_gain, "ft", axis=0, tiled=True),
-        lax.all_gather(feed_shift, "ft", axis=0, tiled=True),
-        lax.all_gather(feed_expand, "ft", axis=0, tiled=True),
-        lax.all_gather(feed_expand_bias, "ft", axis=0, tiled=True),
-        lax.all_gather(feed_reduce, "ft", axis=0, tiled=True),
-        lax.all_gather(feed_reduce_bias, "ft", axis=0, tiled=True),
-    )
+    ) = [wide[i] for i in range(10)]
+    feed_expand_bias = vectors[:, 10:14].reshape(3072)
     time_gain = time_gain.astype(jnp.float32)
     time_shift = time_shift.astype(jnp.float32)
     space_gain = space_gain.astype(jnp.float32)

time: 1190 us -> 1070 us (0.90)
  waiting for transfers between devices: 637 us -> 418 us
  Pallas kernels: 0 us -> 161 us
  blocking collectives: 109 us -> 44.4 us
    all_gather x7 -> x0, waiting for transfers between devices: 223 us -> none  [the longest x1 72.7 us: shards(): lax.all_gather(feed_reduce, 'ft', axis=0, tiled=True)]
    pallas_call x0 -> x1, Pallas kernels: none -> 161 us  [gather(): pl.pallas_call(functools.partial(gather_kernel, count), out_shape=[jax.Sh...]
    all_gather x1 -> x0, blocking collectives: 41.3 us -> none  [shards(): lax.all_gather(feed_expand_bias, 'ft', axis=0, tiled=True)]
    unnamed x2 -> x1, blocking collectives: 45 us -> 22.3 us
    all_to_all x1, waiting for transfers between devices: 0.01 us -> 13 us  [shards(): lax.all_to_all(after_time, 'ft', split_axis=1, concat_axis=2, tiled=True)]
    unnamed x189 -> x171, local copies, waits for them, and re-layouts: 32.1 us -> 31.9 us
  transfers between devices with their start and end apart: 34 -> 27, of which waited for: 23 -> 18; matrix products, arithmetic and copies ran while one was open for 22% -> 14% of each run, Pallas kernels for 0% -> 0%
where the time goes in v1:
time: 1070 us; the launch traced here: 1060 us
  waiting for transfers between devices  418 us (39%)
  Pallas kernels  161 us (15%)
  local copies, waits for them, and re-layouts  154 us (14%)
  matrix products  106 us (10%)
  starting transfers between devices  79.7 us (7%)
  other arithmetic  72.8 us (7%)
  blocking collectives  44.4 us (4%)
  between operations  20.2 us (2%)
    pallas_call x1, Pallas kernels, gather(): pl.pallas_call(functools.partial(gather_kernel, count), out_shape=[jax.Sh...  161 us
    all_to_all x1, waiting for transfers between devices, shards(): lax.all_to_all(blocks[16].astype(jnp.bfloat16), 'ft', split_axis=0, conca...  94.7 us
    all_to_all x1, waiting for transfers between devices, shards(): lax.all_to_all(blocks[14].astype(jnp.bfloat16), 'ft', split_axis=0, conca...  84.8 us
    all_to_all x1, waiting for transfers between devices, shards(): lax.all_to_all(blocks[2].astype(jnp.bfloat16), 'ft', split_axis=0, concat...  69.7 us
    all_to_all x1, waiting for transfers between devices, shards(): lax.all_to_all(blocks[9].astype(jnp.bfloat16), 'ft', split_axis=0, concat...  37.1 us
    dot_general x7, matrix products, matmul(): return jnp.dot(left, right, preferred_element_type=jnp.float32)  36.6 us
    unnamed x171, local copies, waits for them, and re-layouts  31.9 us
    dot_general x7, matrix products, times_transposed(): lax.dot_general(left, right, (((1,), (1,)), ((), ())), preferred_element_...  29.2 us
  transfers between devices with their start and end apart: 27, of which 18 were waited for; matrix products, arithmetic and copies ran while one was open for 14% of the time, Pallas kernels for 0%

profile of v1, /device:TPU:0, one launch (start us, length us, event | category | flops | bytes accessed | tf_op | source)
XLA Modules:
  0.0 1055.1 jit_solution(15846913900852133719)
XLA Ops:
  12.5 160.5 %gather_weights.1 = (bf16[768,2304]{1,0:T(8,128)(2,1)}, bf16[768,768]{1,0:T(8,128)(2,1)}, bf16[768,768]{1,0:T(8,128)(2,1)}, bf16[768,2304]{1,0:T(8,128)(2,1)}, b...) custom-call(bf16[192,2304]{1,0:T(8,128)(2,1)} %refs_0_.1, ...), custom_call_target="tpu_custom_call" | custom-call | tf_op jit(solution)/shard_map/gather_weights/pallas_call | solution.py:207
  179.7 6.5 reshape_reshape.4
  212.6 13.0 %all-to-all-done = bf16[1,8,49,768]{3,2,0,1:T(8,128)(2,1)S(1)} async-done(((bf16[1,8,49,768]{3,2,0,1:T(8,128)(2,1)}), bf16[1,8,49,768]{3,2,0,1:T(8,128)(2,1)S(1)}, u32[]{:S(2)}, u32[]{:S(2)}) %all-to-all-start) | async-done | bytes 602144 | tf_op jit(solution)/shard_map/all_to_all | solution.py:441
  240.3 6.6 reshape.1334
  281.7 9.9 psum.14
  299.0 15.0 %multiply_convert_fusion.1 = (bf16[393,3072]{1,0:T(8,128)(2,1)}, f32[393,3072]{1,0:T(8,128)S(1)}, f32[393,3072]{1,0:T(8,128)S(1)}) fusion(f32[3072]{0:T(1024)S(1)} %reshape.1311, bf16[768,3072]{1,0:T(8,128)(2,1)} %get-tuple-element.36, f32[768]{0:T(1024)S(1)} %reshape.1310, f32[768]{0:T(1024)S(1)} %reshape.1309, f32[393]{0:T(512)S(1)} %add_rsqrt_fusion, ...), kind=kOutput, calls=%fused_computation.15 | convolution fusion | flops 1935899136 | bytes 18020424 | tf_op jit(solution)/shard_map/dot_general | solution.py:231
  314.0 6.4 add_convert_fusion
  360.7 6.5 convert_element_type.754
  367.2 6.2 multiply_reduce_fusion.3
  395.8 9.9 all-to-all-done.1
  416.5 20.3 %all-to-all-done.12 = bf16[4,192,768]{2,1,0:T(8,128)(2,1)} async-done(((bf16[4,192,768]{2,1,0:T(8,128)(2,1)}), bf16[4,192,768]{2,1,0:T(8,128)(2,1)}, u32[]{:S(2)}, u32[]{:S(2)}) %all-to-all-start.12) | async-done | bytes 1179680 | tf_op jit(solution)/shard_map/all_to_all | solution.py:613
  449.3 19.9 %all-to-all-done.7 = bf16[4,192,768]{2,1,0:T(8,128)(2,1)} async-done(((bf16[4,192,768]{2,1,0:T(8,128)(2,1)}), bf16[4,192,768]{2,1,0:T(8,128)(2,1)}, u32[]{:S(2)}, u32[]{:S(2)}) %all-to-all-start.7) | async-done | bytes 1179680 | tf_op jit(solution)/shard_map/all_to_all | solution.py:598
  480.6 20.9 %all-to-all-done.5 = bf16[4,192,768]{2,1,0:T(8,128)(2,1)} async-done(((bf16[4,192,768]{2,1,0:T(8,128)(2,1)}), bf16[4,192,768]{2,1,0:T(8,128)(2,1)}, u32[]{:S(2)}, u32[]{:S(2)}) %all-to-all-start.5) | async-done | bytes 1179680 | tf_op jit(solution)/shard_map/all_to_all | solution.py:592
  524.2 7.0 reshape.1315
  531.3 6.4 convert_element_type.762
  548.1 37.1 %all-to-all-done.11 = bf16[4,192,2304]{2,1,0:T(8,128)(2,1)} async-done(((bf16[4,192,2304]{2,1,0:T(8,128)(2,1)}), bf16[4,192,2304]{2,1,0:T(8,128)(2,1)}, u32[]{:S(2)}, u32[]{:S(2)}) %all-to-all-start.11) | async-done | bytes 3538976 | tf_op jit(solution)/shard_map/all_to_all | solution.py:610
  598.9 69.7 %all-to-all-done.4 = bf16[4,192,2304]{2,1,0:T(8,128)(2,1)} async-done(((bf16[4,192,2304]{2,1,0:T(8,128)(2,1)}), bf16[4,192,2304]{2,1,0:T(8,128)(2,1)}, u32[]{:S(2)}, u32[]{:S(2)}) %all-to-all-start.4) | async-done | bytes 3538976 | tf_op jit(solution)/shard_map/all_to_all | solution.py:589
  692.7 84.8 %all-to-all-done.16 = bf16[4,192,3072]{2,1,0:T(8,128)(2,1)} async-done(((bf16[4,192,3072]{2,1,0:T(8,128)(2,1)}), bf16[4,192,3072]{2,1,0:T(8,128)(2,1)}, u32[]{:S(2)}, u32[]{:S(2)}) %all-to-all-start.16) | async-done | bytes 4718624 | tf_op jit(solution)/shard_map/all_to_all | solution.py:625
  791.8 94.7 %all-to-all-done.18 = bf16[4,768,768]{2,1,0:T(8,128)(2,1)} async-done(((bf16[4,768,768]{2,1,0:T(8,128)(2,1)}), bf16[4,768,768]{2,1,0:T(8,128)(2,1)}, u32[]{:S(2)}, u32[]{:S(2)}) %all-to-all-start.18) | async-done | bytes 4718624 | tf_op jit(solution)/shard_map/all_to_all | solution.py:631
  907.8 12.2 %psum.15 = f32[1,768]{1,0:T(1,128)S(1)} all-reduce(f32[1,768]{1,0:T(1,128)S(1)} %reduce_sum.618), channel_id=1, replica_groups=mesh['seq'=8,'ft'=4] {'ft'}, use_global_device_ids=true, to_apply=%region_27.28 | all-reduce | flops 768 | bytes 6144 | tf_op jit(solution)/shard_map/psum | solution.py:531
  938.1 5.5 all-to-all-done.15
  973.2 5.5 all-to-all-done.17
  995.9 5.5 all-to-all-done.6
  1019.0 22.3 %all-reduce.12 = (f32[192]{0:T(256)S(1)}, f32[192]{0:T(256)S(1)}, f32[192]{0:T(256)S(1)}, f32[192]{0:T(256)S(1)}, f32[192]{0:T(256)S(1)}, /*index=5*/f32[192]{0:...) all-reduce(f32[192]{0:T(256)S(1)} %convert_reduce_fusion.18, ...), channel_id=2, replica_groups=mesh['seq'=8,'ft'=4] {'seq'}, use_global_device_ids=true, to_apply=%region_30.31.clone | all-reduce | flops 2688 | bytes 21504
  (471 shorter events, 382.4 us)
Async XLA Ops:
  201.9 23.7 %all-to-all-start = ((bf16[1,8,49,768]{3,2,0,1:T(8,128)(2,1)}), bf16[1,8,49,768]{3,2,0,1:T(8,128)(2,1)S(1)}, u32[]{:S(2)}, u32[]{:S(2)}) async-start(bf16[1,8,49,768]{3,2,0,1:T(8,128)(2,1)} %bitcast.8), calls=%async_computation | async-start | bytes 1376256 | tf_op jit(solution)/shard_map/all_to_all | solution.py:441
  387.4 18.2 %all-to-all-start.1 = ((bf16[1,2,196,768]{3,1,0,2:T(2,128)(2,1)}), bf16[1,2,196,768]{3,1,0,2:T(2,128)(2,1)}, u32[]{:S(2)}, u32[]{:S(2)}) async-start(bf16[1,2,196,768]{3,1,0,2:T(2,128)(2,1)} %fusion.63), calls=%async_computation.1 | async-start | bytes 1204224 | tf_op jit(solution)/shard_map/all_to_all | solution.py:536
  405.6 31.1 %all-to-all-start.12 = ((bf16[4,192,768]{2,1,0:T(8,128)(2,1)}), bf16[4,192,768]{2,1,0:T(8,128)(2,1)}, u32[]{:S(2)}, u32[]{:S(2)}) async-start(bf16[4,192,768]{2,1,0:T(8,128)(2,1)} %bitcast.220), calls=%async_computation.16 | async-start | bytes 2359296 | tf_op jit(solution)/shard_map/all_to_all | solution.py:613
  436.8 32.4 %all-to-all-start.7 = ((bf16[4,192,768]{2,1,0:T(8,128)(2,1)}), bf16[4,192,768]{2,1,0:T(8,128)(2,1)}, u32[]{:S(2)}, u32[]{:S(2)}) async-start(bf16[4,192,768]{2,1,0:T(8,128)(2,1)} %bitcast.219), calls=%async_computation.9 | async-start | bytes 2359296 | tf_op jit(solution)/shard_map/all_to_all | solution.py:598
  469.2 32.4 %all-to-all-start.5 = ((bf16[4,192,768]{2,1,0:T(8,128)(2,1)}), bf16[4,192,768]{2,1,0:T(8,128)(2,1)}, u32[]{:S(2)}, u32[]{:S(2)}) async-start(bf16[4,192,768]{2,1,0:T(8,128)(2,1)} %bitcast.221), calls=%async_computation.6 | async-start | bytes 2359296 | tf_op jit(solution)/shard_map/all_to_all | solution.py:592
  501.5 83.7 %all-to-all-start.11 = ((bf16[4,192,2304]{2,1,0:T(8,128)(2,1)}), bf16[4,192,2304]{2,1,0:T(8,128)(2,1)}, u32[]{:S(2)}, u32[]{:S(2)}) async-start(bf16[4,192,2304]{2,1,0:T(8,128)(2,1)} %bitcast.214), calls=%async_computation.14 | async-start | bytes 7077888 | tf_op jit(solution)/shard_map/all_to_all | solution.py:610
  585.2 83.4 %all-to-all-start.4 = ((bf16[4,192,2304]{2,1,0:T(8,128)(2,1)}), bf16[4,192,2304]{2,1,0:T(8,128)(2,1)}, u32[]{:S(2)}, u32[]{:S(2)}) async-start(bf16[4,192,2304]{2,1,0:T(8,128)(2,1)} %bitcast.50), calls=%async_computation.4 | async-start | bytes 7077888 | tf_op jit(solution)/shard_map/all_to_all | solution.py:589
  668.6 108.9 %all-to-all-start.16 = ((bf16[4,192,3072]{2,1,0:T(8,128)(2,1)}), bf16[4,192,3072]{2,1,0:T(8,128)(2,1)}, u32[]{:S(2)}, u32[]{:S(2)}) async-start(bf16[4,192,3072]{2,1,0:T(8,128)(2,1)} %bitcast.212), calls=%async_computation.21 | async-start | bytes 9437184 | tf_op jit(solution)/shard_map/all_to_all | solution.py:625
  673.6 374.2 %reduce-scatter.16.cloned.1.call-start = ((), (), s32[]{:S(2)}) async-start(), calls=%async_computation.31 | async-start | bytes 663552 | tf_op jit(solution)/shard_map/reduce_scatter | solution.py:650
  676.0 371.8 %reduce-scatter.12.cloned.1.call-start = ((), (), s32[]{:S(2)}) async-start(), calls=%async_computation.29 | async-start | bytes 663552 | tf_op jit(solution)/shard_map/reduce_scatter | solution.py:645
  678.3 369.4 %reduce-scatter.10.cloned.1.call-start = ((), (), s32[]{:S(2)}) async-start(), calls=%async_computation.28 | async-start | bytes 663552 | tf_op jit(solution)/shard_map/reduce_scatter | solution.py:643
  680.7 367.0 %reduce-scatter.14.cloned.1.call-start = ((), (), s32[]{:S(2)}) async-start(), calls=%async_computation.30 | async-start | bytes 1990656 | tf_op jit(solution)/shard_map/reduce_scatter | solution.py:649
  777.5 109.0 %all-to-all-start.18 = ((bf16[4,768,768]{2,1,0:T(8,128)(2,1)}), bf16[4,768,768]{2,1,0:T(8,128)(2,1)}, u32[]{:S(2)}, u32[]{:S(2)}) async-start(bf16[4,768,768]{2,1,0:T(8,128)(2,1)} %bitcast.213), calls=%async_computation.24 | async-start | bytes 9437184 | tf_op jit(solution)/shard_map/all_to_all | solution.py:631
  782.5 265.3 %reduce-scatter.8.cloned.1.call-start = ((), (), s32[]{:S(2)}) async-start(), calls=%async_computation.27 | async-start | bytes 1990656 | tf_op jit(solution)/shard_map/reduce_scatter | solution.py:642
  786.8 261.1 %reduce-scatter.18.cloned.1.call-start = ((), (), s32[]{:S(2)}) async-start(), calls=%async_computation.32 | async-start | bytes 2654208 | tf_op jit(solution)/shard_map/reduce_scatter | solution.py:654
  791.8 256.1 %reduce-scatter.20.cloned.1.call-start = ((), (), s32[]{:S(2)}) async-start(), calls=%async_computation.33 | async-start | bytes 2654208 | tf_op jit(solution)/shard_map/reduce_scatter | solution.py:656
  903.7 31.2 %all-to-all-start.14 = ((bf16[4,1,192]{2,1,0:T(2,128)(2,1)}), bf16[4,1,192]{2,1,0:T(2,128)(2,1)S(1)}, u32[]{:S(2)}, u32[]{:S(2)}) async-start(bf16[4,1,192]{2,1,0:T(2,128)(2,1)} %convert_element_type.866), calls=%async_computation.19 | async-start | bytes 8192 | tf_op jit(solution)/shard_map/all_to_all | solution.py:619
  934.9 8.8 all-to-all-start.15
  952.3 8.8 all-to-all-start.10
  961.1 8.8 all-to-all-start.9
  969.9 8.8 all-to-all-start.17
  981.2 9.7 all-to-all-start.8
  990.8 10.6 %all-to-all-start.6 = ((bf16[4,1,192]{2,1,0:T(2,128)(2,1)}), bf16[4,1,192]{2,1,0:T(2,128)(2,1)S(1)}, u32[]{:S(2)}, u32[]{:S(2)}) async-start(bf16[4,1,192]{2,1,0:T(2,128)(2,1)} %convert_element_type.861), calls=%async_computation.8 | async-start | bytes 8192 | tf_op jit(solution)/shard_map/all_to_all | solution.py:595
  1010.2 8.8 all-to-all-start.2
  (77 other events, 855.3 us)
Sparse Core Ops, SparseCore 0:
  678.1 34.9 reduce-scatter.15
  716.8 34.3 reduce-scatter.11
  754.9 34.3 reduce-scatter.9
  793.1 39.4 reduce-scatter.13
  836.4 39.4 reduce-scatter.7
  879.6 42.4 reduce-scatter.17
  926.4 42.4 reduce-scatter.19

commit v2 on v1

--- a/solution.py
+++ b/solution.py
@@ -213,6 +213,185 @@
         compiler_params=pltpu.CompilerParams(collective_id=1, has_side_effects=True),
         name="gather_weights",
     )(*shards)
+
+
+class Reduce:
+    def __init__(self, parts, outs, scratch):
+        self.parts, self.outs = parts, outs
+        (self.ra, self.rb, self.ra2, self.rb2, self.sz, self.rz, self.total, self.rc) = scratch[:8]
+        self.sems = scratch[8]
+        self.s, self.f, self.core, self.col, self.row = place()
+        self.sib, self.across, self.down = peers(self.s, self.core, self.col, self.row)
+
+    def greet(self):
+        bar = pltpu.get_barrier_semaphore()
+        f = self.f
+        targets = [(t, f) for t in (self.sib, self.across, self.down)]
+        targets += [(self.s, lax.rem(f + j, 4)) for j in (1, 2, 3)]
+        for t in targets:
+            pl.semaphore_signal(bar, inc=1, device_id=t, device_id_type=MESH)
+        pl.semaphore_wait(bar, len(targets))
+
+    def sem(self, w, i):
+        return self.sems.at[w, i]
+
+    def copies1(self, w):
+        g = self.parts[w]
+        rows = self.ra[w].shape[1]
+        return (
+            remote(g.at[:, 1 - self.col, 0], self.ra[w], self.sem(w, 0), self.sem(w, 1), (self.across, self.f)),
+            remote(g.at[1 - self.row, :, 1], self.rb[w], self.sem(w, 2), self.sem(w, 3), (self.down, self.f)),
+        )
+
+    def copies2(self, w):
+        return (
+            remote(self.ra[w].at[1 - self.row], self.ra2[w], self.sem(w, 4), self.sem(w, 5), (self.down, self.f)),
+            remote(self.rb[w].at[1 - self.col], self.rb2[w], self.sem(w, 6), self.sem(w, 7), (self.across, self.f)),
+        )
+
+    def copies3(self, w):
+        out = []
+        for j in (1, 2, 3):
+            z = lax.rem(self.f + j, 4)
+            out.append(
+                remote(self.sz[w].at[z], self.rz[w].at[3 - j], self.sem(w, 7 + j), self.sem(w, 14 - j), (self.s, z))
+            )
+        return out
+
+    def copies4(self, w):
+        return remote(self.total[w].at[1 - self.core], self.rc[w], self.sem(w, 14), self.sem(w, 15), (self.sib, self.f))
+
+    def step1(self, w):
+        for c in self.copies1(w):
+            c.start()
+
+    def step2(self, w):
+        a, b = self.copies1(w)
+        g, ra, rb = self.parts[w], self.ra[w], self.rb[w]
+        row, col = self.row, self.col
+        a2, b2 = self.copies2(w)
+        a.wait_recv()
+        ra[1 - row] = (ra[1 - row].astype(jnp.float32) + g[1 - row, col, 0].astype(jnp.float32)).astype(jnp.bfloat16)
+        a2.start()
+        b.wait_recv()
+        rb[1 - col] = (rb[1 - col].astype(jnp.float32) + g[row, 1 - col, 1].astype(jnp.float32)).astype(jnp.bfloat16)
+        b2.start()
+
+    def step3(self, w):
+        a2, b2 = self.copies2(w)
+        g, ra, rb = self.parts[w], self.ra[w], self.rb[w]
+        row, col = self.row, self.col
+        part = self.sz[w].shape[2]
+        b2.wait_recv()
+        a2.wait_recv()
+        for z in range(4):
+            rows = pl.ds(z * part, part)
+            for k, near, far in ((0, ra.at[row], self.ra2[w]), (1, rb.at[col], self.rb2[w])):
+                own = g.at[row, col, k]
+                self.sz[w][z, k] = (
+                    own[rows].astype(jnp.float32) + near[rows].astype(jnp.float32) + far[rows].astype(jnp.float32)
+                ).astype(jnp.bfloat16)
+        for c in self.copies3(w):
+            c.start()
+
+    def step4(self, w):
+        for c in self.copies3(w):
+            c.wait_recv()
+        rz = self.rz[w]
+        self.total[w][...] = (
+            (self.sz[w][self.f].astype(jnp.float32) + rz[0].astype(jnp.float32))
+            + (rz[1].astype(jnp.float32) + rz[2].astype(jnp.float32))
+        )
+        self.copies4(w).start()
+        half = self.rc[w].shape[1]
+        self.outs[w][:, pl.ds(pl.multiple_of(self.core * half, 128), half)] = self.total[w][self.core]
+
+    def step5(self, w):
+        self.copies4(w).wait_recv()
+        half = self.rc[w].shape[1]
+        self.outs[w][:, pl.ds(pl.multiple_of((1 - self.core) * half, 128), half)] = self.rc[w][...]
+
+    def drain(self, w):
+        for c in self.copies1(w) + self.copies2(w) + tuple(self.copies3(w)) + (self.copies4(w),):
+            c.wait_send()
+
+
+def scratch_of(shapes):
+    bf, f32 = jnp.bfloat16, jnp.float32
+    v = pltpu.VMEM
+    return [
+        [v((2, k // 8, h), bf) for k, h in shapes],
+        [v((2, k // 8, h), bf) for k, h in shapes],
+        [v((k // 8, h), bf) for k, h in shapes],
+        [v((k // 8, h), bf) for k, h in shapes],
+        [v((4, 2, k // 32, h), bf) for k, h in shapes],
+        [v((3, 2, k // 32, h), bf) for k, h in shapes],
+        [v((2, k // 32, h), f32) for k, h in shapes],
+        [v((k // 32, h), f32) for k, h in shapes],
+        pltpu.SemaphoreType.DMA((len(shapes), 16)),
+    ]
+
+
+def reduce_kernel(count, *refs):
+    red = Reduce(refs[:count], refs[count : 2 * count], refs[2 * count :])
+    red.greet()
+    steps = (red.step1, red.step2, red.step3, red.step4, red.step5)
+    for t in range(count + len(steps) - 1):
+        for k, step in enumerate(steps):
+            if 0 <= t - k < count:
+                step(t - k)
+    for w in range(count):
+        red.drain(w)
+
+
+def reduce_scatter(parts):
+    count = len(parts)
+    shapes = [(p.shape[0] * p.shape[1] * p.shape[2] * p.shape[3], p.shape[4]) for p in parts]
+    vm = pl.BlockSpec(memory_space=pltpu.VMEM)
+    return pl.pallas_call(
+        functools.partial(reduce_kernel, count),
+        out_shape=[jax.ShapeDtypeStruct((k // 32, 2 * h), jnp.float32) for k, h in shapes],
+        in_specs=[vm] * count,
+        out_specs=[vm] * count,
+        scratch_shapes=scratch_of(shapes),
+        compiler_params=pltpu.CompilerParams(collective_id=2, has_side_effects=True, vmem_limit_bytes=60 << 20),
+        name="reduce_gradients",
+    )(*parts)
+
+
+def swap(values):
+    count = lax.axis_size("seq")
+    return lax.ppermute(values, "seq", [(i, i ^ 1) for i in range(count)])
+
+
+def half_gradient(left, right):
+    core = lax.rem(lax.axis_index("seq"), 2)
+    half = right.shape[1] // 2
+    mine = lax.dynamic_slice_in_dim(right, core * half, half, 1)
+    theirs = lax.dynamic_slice_in_dim(right, (1 - core) * half, half, 1)
+    both_left = jnp.concatenate([left, swap(left)], axis=0)
+    both_right = jnp.concatenate([mine, swap(theirs)], axis=0)
+    return (
+        transposed_times(both_left, both_right)
+        .astype(jnp.bfloat16)
+        .reshape(2, 2, 2, left.shape[1] // 8, half)
+    )
+
+
+def settle(share):
+    count = lax.axis_size("seq")
+    if count == 8:
+        return share
+    more = count // 8
+    groups = [[low + 8 * high for high in range(more)] for low in range(8)]
+    share = lax.psum_scatter(share, "seq", scatter_dimension=0, tiled=True, axis_index_groups=groups)
+    moves = [
+        ((high * 8 + low) * 4 + f, (low * 4 + f) * more + high)
+        for high in range(more)
+        for low in range(8)
+        for f in range(4)
+    ]
+    return lax.ppermute(share, ("seq", "ft"), moves)
 
 
 def layer_norm(values, gain, shift):
@@ -484,7 +663,7 @@
     grad_patch_rows = grad_output.reshape(patch_count, width)
     grad_result = jnp.concatenate([grad_patch_rows, grad_class_out], axis=0)
     grad_counted = jnp.concatenate([grad_patch_rows, grad_class_out * first], axis=0)
-    grad_feed_reduce = transposed_times(active, grad_counted)
+    grad_feed_reduce = half_gradient(active, grad_counted)
     grad_feed_reduce_bias = column_sum(grad_counted)
     grad_active = times_transposed(grad_result, feed_reduce)
     unused, gelu_pull = jax.vjp(partial(jax.nn.gelu, approximate=False), hidden)
@@ -492,7 +671,7 @@
     hidden_counted = jnp.concatenate(
         [grad_hidden[:patch_count], grad_hidden[patch_count:] * first], axis=0
     )
-    grad_feed_expand = transposed_times(feed_normed, hidden_counted)
+    grad_feed_expand = half_gradient(feed_normed, hidden_counted)
     grad_feed_expand_bias = column_sum(hidden_counted)
     grad_feed_normed = times_transposed(grad_hidden, feed_expand)
     patch_grad, gain_patch, shift_patch = norm_pull(
@@ -515,13 +694,13 @@
         axis=2,
     ).astype(jnp.bfloat16)
     grad_branch_rows = grad_branch.reshape(-1, width)
-    grad_space_output = transposed_times(space_mixed.reshape(-1, width), grad_branch_rows)
+    grad_space_output = half_gradient(space_mixed.reshape(-1, width), grad_branch_rows)
     grad_space_output_bias = column_sum(grad_branch_rows)
     grad_space_mixed = times_transposed(grad_branch_rows, space_output).astype(jnp.bfloat16)
     grad_space_joined = attend_backward(
         space_joined, space_allowed, space_total, grad_space_mixed, "abl"
     ).reshape(-1, 3 * width)
-    grad_space_project = transposed_times(space_normed.reshape(-1, width), grad_space_joined)
+    grad_space_project = half_gradient(space_normed.reshape(-1, width), grad_space_joined)
     grad_space_normed = times_transposed(grad_space_joined, space_project).reshape(
         seqs_here, frames_here, length, width
     )
@@ -537,16 +716,16 @@
         grad_after_space, "ft", split_axis=2, concat_axis=1, tiled=True
     )
     grad_time_branch = grad_after_time.reshape(total_rows, width)
-    grad_time_mixer = transposed_times(time_outer, grad_time_branch)
+    grad_time_mixer = half_gradient(time_outer, grad_time_branch)
     grad_time_mixer_bias = column_sum(grad_time_branch)
     grad_time_outer = times_transposed(grad_time_branch, time_mixer).astype(jnp.bfloat16)
-    grad_time_output = transposed_times(time_mixed.reshape(total_rows, width), grad_time_outer)
+    grad_time_output = half_gradient(time_mixed.reshape(total_rows, width), grad_time_outer)
     grad_time_output_bias = column_sum(grad_time_outer)
     grad_time_mixed = times_transposed(grad_time_outer, time_output).astype(jnp.bfloat16)
     grad_time_joined = attend_backward(
         time_joined, time_allowed, time_total, grad_time_mixed, "alb"
     ).reshape(total_rows, 3 * width)
-    grad_time_project = transposed_times(time_normed, grad_time_joined)
+    grad_time_project = half_gradient(time_normed, grad_time_joined)
     grad_time_normed = times_transposed(grad_time_joined, time_project)
     grad_time_rows, grad_time_gain, grad_time_shift = norm_pull(
         time_rows, time_gain, time_shift, grad_time_normed
@@ -554,107 +733,68 @@
     grad_video = (grad_time_branch.astype(jnp.float32) + grad_time_rows).reshape(
         seqs_here, frames, patch_here, width
     )
-    local = (
-        grad_time_gain,
-        grad_time_shift,
+    narrow = jnp.stack(
+        [
+            grad_time_gain,
+            grad_time_shift,
+            grad_time_output_bias,
+            grad_time_mixer_bias,
+            grad_space_gain,
+            grad_space_shift,
+            grad_space_output_bias,
+            grad_feed_gain,
+            grad_feed_shift,
+            grad_feed_reduce_bias,
+        ],
+        axis=1,
+    )
+    narrow = jnp.concatenate([narrow, grad_feed_expand_bias.reshape(768, 4)], axis=1)
+    narrow = jnp.pad(narrow + swap(narrow), ((0, 0), (0, 242)))
+    core = lax.rem(lax.axis_index("seq"), 2)
+    narrow = lax.dynamic_slice_in_dim(narrow, core * 128, 128, 1).astype(jnp.bfloat16)
+    (
+        grad_feed_reduce,
+        grad_feed_expand,
+        grad_space_output,
+        grad_space_project,
+        grad_time_mixer,
+        grad_time_output,
+        grad_time_project,
+        narrow,
+    ) = [
+        settle(item)
+        for item in reduce_scatter(
+            (
+                grad_feed_reduce,
+                grad_feed_expand,
+                grad_space_output,
+                grad_space_project,
+                grad_time_mixer,
+                grad_time_output,
+                grad_time_project,
+                narrow.reshape(2, 2, 2, 96, 128),
+            )
+        )
+    ]
+    shares = (
+        narrow[:, 0],
+        narrow[:, 1],
         grad_time_project,
         grad_time_output,
-        grad_time_output_bias,
+        narrow[:, 2],
         grad_time_mixer,
-        grad_time_mixer_bias,
-        grad_space_gain,
-        grad_space_shift,
+        narrow[:, 3],
+        narrow[:, 4],
+        narrow[:, 5],
         grad_space_project,
         grad_space_output,
-        grad_space_output_bias,
-        grad_feed_gain,
-        grad_feed_shift,
+        narrow[:, 6],
+        narrow[:, 7],
+        narrow[:, 8],
         grad_feed_expand,
-        grad_feed_expand_bias,
+        narrow[:, 10:14].reshape(-1),
         grad_feed_reduce,
-        grad_feed_reduce_bias,
-    )
-    seq_count = lax.axis_size("seq")
-    ft_count = lax.axis_size("ft")
-    blocks = tuple(
-        (row_blocks(reorder_rows(item, seq_count, ft_count), ft_count) for item in local)
-    )
-    moved = (
-        lax.all_to_all(
-            blocks[0].astype(jnp.bfloat16), "ft", split_axis=0, concat_axis=0, tiled=True
-        ).astype(jnp.float32),
-        lax.all_to_all(
-            blocks[1].astype(jnp.bfloat16), "ft", split_axis=0, concat_axis=0, tiled=True
-        ).astype(jnp.float32),
-        lax.all_to_all(
-            blocks[2].astype(jnp.bfloat16), "ft", split_axis=0, concat_axis=0, tiled=True
-        ).astype(jnp.float32),
-        lax.all_to_all(
-            blocks[3].astype(jnp.bfloat16), "ft", split_axis=0, concat_axis=0, tiled=True
-        ).astype(jnp.float32),
-        lax.all_to_all(
-            blocks[4].astype(jnp.bfloat16), "ft", split_axis=0, concat_axis=0, tiled=True
-        ).astype(jnp.float32),
-        lax.all_to_all(
-            blocks[5].astype(jnp.bfloat16), "ft", split_axis=0, concat_axis=0, tiled=True
-        ).astype(jnp.float32),
-        lax.all_to_all(
-            blocks[6].astype(jnp.bfloat16), "ft", split_axis=0, concat_axis=0, tiled=True
-        ).astype(jnp.float32),
-        lax.all_to_all(
-            blocks[7].astype(jnp.bfloat16), "ft", split_axis=0, concat_axis=0, tiled=True
-        ).astype(jnp.float32),
-        lax.all_to_all(
-            blocks[8].astype(jnp.bfloat16), "ft", split_axis=0, concat_axis=0, tiled=True
-        ).astype(jnp.float32),
-        lax.all_to_all(
-            blocks[9].astype(jnp.bfloat16), "ft", split_axis=0, concat_axis=0, tiled=True
-        ).astype(jnp.float32),
-        lax.all_to_all(
-            blocks[10].astype(jnp.bfloat16), "ft", split_axis=0, concat_axis=0, tiled=True
-        ).astype(jnp.float32),
-        lax.all_to_all(
-            blocks[11].astype(jnp.bfloat16), "ft", split_axis=0, concat_axis=0, tiled=True
-        ).astype(jnp.float32),
-        lax.all_to_all(
-            blocks[12].astype(jnp.bfloat16), "ft", split_axis=0, concat_axis=0, tiled=True
-        ).astype(jnp.float32),
-        lax.all_to_all(
-            blocks[13].astype(jnp.bfloat16), "ft", split_axis=0, concat_axis=0, tiled=True
-        ).astype(jnp.float32),
-        lax.all_to_all(
-            blocks[14].astype(jnp.bfloat16), "ft", split_axis=0, concat_axis=0, tiled=True
-        ).astype(jnp.float32),
-        lax.all_to_all(
-            blocks[15].astype(jnp.bfloat16), "ft", split_axis=0, concat_axis=0, tiled=True
-        ).astype(jnp.float32),
-        lax.all_to_all(
-            blocks[16].astype(jnp.bfloat16), "ft", split_axis=0, concat_axis=0, tiled=True
-        ).astype(jnp.float32),
-        lax.all_to_all(
-            blocks[17].astype(jnp.bfloat16), "ft", split_axis=0, concat_axis=0, tiled=True
-        ).astype(jnp.float32),
-    )
-    summed = tuple((jnp.sum(item, axis=0) for item in moved))
-    shares = (
-        lax.psum_scatter(summed[0], "seq", scatter_dimension=0, tiled=True),
-        lax.psum_scatter(summed[1], "seq", scatter_dimension=0, tiled=True),
-        lax.psum_scatter(summed[2], "seq", scatter_dimension=0, tiled=True),
-        lax.psum_scatter(summed[3], "seq", scatter_dimension=0, tiled=True),
-        lax.psum_scatter(summed[4], "seq", scatter_dimension=0, tiled=True),
-        lax.psum_scatter(summed[5], "seq", scatter_dimension=0, tiled=True),
-        lax.psum_scatter(summed[6], "seq", scatter_dimension=0, tiled=True),
-        lax.psum_scatter(summed[7], "seq", scatter_dimension=0, tiled=True),
-        lax.psum_scatter(summed[8], "seq", scatter_dimension=0, tiled=True),
-        lax.psum_scatter(summed[9], "seq", scatter_dimension=0, tiled=True),
-        lax.psum_scatter(summed[10], "seq", scatter_dimension=0, tiled=True),
-        lax.psum_scatter(summed[11], "seq", scatter_dimension=0, tiled=True),
-        lax.psum_scatter(summed[12], "seq", scatter_dimension=0, tiled=True),
-        lax.psum_scatter(summed[13], "seq", scatter_dimension=0, tiled=True),
-        lax.psum_scatter(summed[14], "seq", scatter_dimension=0, tiled=True),
-        lax.psum_scatter(summed[15], "seq", scatter_dimension=0, tiled=True),
-        lax.psum_scatter(summed[16], "seq", scatter_dimension=0, tiled=True),
-        lax.psum_scatter(summed[17], "seq", scatter_dimension=0, tiled=True),
+        narrow[:, 9],
     )
     return (output, class_output, grad_video, grad_class) + tuple(shares)
 

time: 1070 us -> 649 us (0.61)
  waiting for transfers between devices: 418 us -> 8.56 us
  Pallas kernels: 161 us -> 266 us
  starting transfers between devices: 79.7 us -> 12.2 us
  blocking collectives: 44.4 us -> 21.8 us
  other arithmetic: 72.8 us -> 52.3 us
  between operations: 20.2 us -> 5.1 us
    all_to_all x18 -> x0, waiting for transfers between devices: 395 us -> none  [the longest x1 94.7 us: shards(): lax.all_to_all(blocks[16].astype(jnp.bfloat16), 'ft', split_axis=0, conca...]
    pallas_call x0 -> x1, Pallas kernels: none -> 105 us  [reduce_scatter(): pl.pallas_call(functools.partial(reduce_kernel, count), out_shape=[jax.Sh...]
    all_to_all x18 -> x0, starting transfers between devices: 70 us -> none  [the longest x1 5.04 us: shards(): lax.all_to_all(blocks[4].astype(jnp.bfloat16), 'ft', split_axis=0, concat...]
    reduce_sum x18 -> x0, other arithmetic: 25 us -> none  [shards(): summed = tuple((jnp.sum(item, axis=0) for item in moved))]
    unnamed x1 -> x0, blocking collectives: 22.3 us -> none
    convert_element_type x40 -> x2, local copies, waits for them, and re-layouts: 21.9 us -> 0.84 us  [shards(): lax.dynamic_slice_in_dim(narrow, core * 128, 128, 1).astype(jnp.bfloat16)]
    convert_element_type x5 -> x2, local copies, waits for them, and re-layouts: 26.8 us -> 13.1 us  [attend_backward(): return stacked.reshape(joined.shape).astype(jnp.bfloat16)]
    dot_general x7, matrix products: 20 us -> 32.7 us  [transposed_times(): lax.dot_general(left, right, (((0,), (0,)), ((), ())), preferred_element_...]
  transfers between devices with their start and end apart: 27 -> 17, of which waited for: 18 -> 1; matrix products, arithmetic and copies ran while one was open for 14% -> 42% of each run, Pallas kernels for 0% -> 0%
where the time goes in v2:
time: 649 us; the launch traced here: 636 us
  Pallas kernels  266 us (41%)
  local copies, waits for them, and re-layouts  156 us (24%)
  matrix products  115 us (18%)
  other arithmetic  52.3 us (8%)
  blocking collectives  21.8 us (3%)
  starting transfers between devices  12.2 us (2%)
  waiting for transfers between devices  8.56 us (1%)
    pallas_call x1, Pallas kernels, gather(): pl.pallas_call(functools.partial(gather_kernel, count), out_shape=[jax.Sh...  160 us
    pallas_call x1, Pallas kernels, reduce_scatter(): pl.pallas_call(functools.partial(reduce_kernel, count), out_shape=[jax.Sh...  105 us
    dot_general x7, matrix products, matmul(): return jnp.dot(left, right, preferred_element_type=jnp.float32)  37.5 us
    unnamed x232, local copies, waits for them, and re-layouts  32.8 us
    dot_general x7, matrix products, transposed_times(): lax.dot_general(left, right, (((0,), (0,)), ((), ())), preferred_element_...  32.7 us
    dot_general x7, matrix products, times_transposed(): lax.dot_general(left, right, (((1,), (1,)), ((), ())), preferred_element_...  26.5 us
    convert_element_type x2, local copies, waits for them, and re-layouts, attend_backward(): return stacked.reshape(joined.shape).astype(jnp.bfloat16)  13.1 us
  transfers between devices with their start and end apart: 17, of which 1 were waited for; matrix products, arithmetic and copies ran while one was open for 42% of the time, Pallas kernels for 0%

profile of v2, /device:TPU:0, one launch (start us, length us, event | category | flops | bytes accessed | tf_op | source)
XLA Modules:
  0.0 636.5 jit_solution(18034050087147833471)
XLA Ops:
  4.6 160.4 %gather_weights.1 = (bf16[768,2304]{1,0:T(8,128)(2,1)}, bf16[768,768]{1,0:T(8,128)(2,1)}, bf16[768,768]{1,0:T(8,128)(2,1)}, bf16[768,2304]{1,0:T(8,128)(2,1)}, b...) custom-call(bf16[192,2304]{1,0:T(8,128)(2,1)} %refs_0_.1, ...), custom_call_target="tpu_custom_call" | custom-call | tf_op jit(solution)/shard_map/gather_weights/pallas_call | solution.py:207
  171.6 5.1 reshape_reshape.8
  195.9 4.9 all-to-all-start
  211.1 8.5 %all-to-all-done = bf16[1,8,49,768]{3,2,0,1:T(8,128)(2,1)} async-done(((bf16[1,8,49,768]{3,2,0,1:T(8,128)(2,1)}), bf16[1,8,49,768]{3,2,0,1:T(8,128)(2,1)}, u32[]{:S(2)}, u32[]{:S(2)}) %all-to-all-start) | async-done | bytes 602144 | tf_op jit(solution)/shard_map/all_to_all | solution.py:620
  232.2 5.1 convolution_convert_fusion
  237.2 6.6 %reshape.1086 = bf16[1,2,197,3,12,64]{5,4,3,2,1,0:T(8,128)(2,1)} reshape(bf16[394,2304]{1,0:T(8,128)(2,1)} %convolution_convert_fusion) | data formatting | bytes 3631104 | tf_op jit(solution)/shard_map/reshape;reshape | solution.py:442
  243.9 5.0 fusion.140
  282.9 9.8 %psum.14 = f32[1,768]{1,0:T(1,128)S(1)} all-reduce(f32[1,768]{1,0:T(1,128)S(1)} %reduce_sum.336), channel_id=1, replica_groups=mesh['seq'=8,'ft'=4] {'ft'}, use_global_device_ids=true, to_apply=%region_9.10 | all-reduce | flops 768 | bytes 6144 | tf_op jit(solution)/shard_map/psum | solution.py:649
  295.4 14.9 %multiply_convert_fusion.1 = (bf16[393,3072]{1,0:T(8,128)(2,1)}, f32[393,3072]{1,0:T(8,128)S(1)}, f32[393,3072]{1,0:T(8,128)S(1)}) fusion(f32[3072]{0:T(1024)S(1)} %copy-done.84, bf16[393,768]{1,0:T(8,128)(2,1)S(1)} %add_convert_fusion.1, bf16[768,3072]{1,0:T(8,128)(2,1)} %get-tuple-element.44), kind=kOutput, calls=%fused_computation.7 | convolution fusion | flops 1934088192 | bytes 17407488 | tf_op jit(solution)/shard_map/dot_general | solution.py:410
  310.3 4.1 add_convert_fusion
  316.0 5.7 fusion.145
  352.1 4.2 multiply_reduce_fusion
  361.2 3.9 copy.243
  365.1 6.5 %convert_element_type.418 = bf16[394,2304]{0,1:T(8,128)(2,1)} reshape(bf16[1,2,197,3,12,64]{2,1,5,4,3,0:T(2,128)(2,1)} %copy.243) | data formatting | bytes 3631104 | tf_op jit(solution)/shard_map/convert_element_type | solution.py:503
  371.6 6.2 multiply_reduce_fusion.3
  385.5 4.9 fusion.65
  392.1 5.3 fusion.44
  411.9 12.0 %psum.15 = f32[1,768]{1,0:T(1,128)S(1)} all-reduce(f32[1,768]{1,0:T(1,128)S(1)} %reduce_sum.370), channel_id=1, replica_groups=mesh['seq'=8,'ft'=4] {'ft'}, use_global_device_ids=true, to_apply=%region_27.28 | all-reduce | flops 768 | bytes 6144 | tf_op jit(solution)/shard_map/psum | solution.py:710
  464.0 6.6 %convert_element_type.425 = bf16[392,2304]{1,0:T(8,128)(2,1)S(1)} reshape(bf16[1,8,49,3,12,64]{5,4,3,2,1,0:T(8,128)(2,1)} %copy.254) | data formatting | bytes 3612672 | tf_op jit(solution)/shard_map/convert_element_type | solution.py:503
  487.6 5.1 convolution_convert_fusion.3
  500.7 5.7 convolution_convert_fusion.4
  506.4 4.6 convolution_convert_fusion.2
  511.0 7.4 %fusion.11 = bf16[3072,384]{1,0:T(8,128)(2,1)} fusion(bf16[393,3072]{1,0:T(8,128)(2,1)} %collective-permute-done, bf16[393,3072]{1,0:T(8,128)(2,1)} %get-tuple-element.207, bf16[393,384]{1,0:T(8,128)(2,1)S(1)} %collective-permute-done.1, bf16[393,384]{1,0:T(8,128)(2,1)S(1)} %copy-done.47), kind=kOutput, calls=%fused_computation.34 | convolution fusion | flops 1866451968 | bytes 7792128 | tf_op jit(solution)/shard_map/dot_general | solution.py:420
  518.5 105.1 %reduce_gradients.1 = (f32[96,768]{1,0:T(8,128)}, f32[24,3072]{1,0:T(8,128)}, f32[24,768]{1,0:T(8,128)}, f32[24,2304]{1,0:T(8,128)}, f32[24,768]{1,0:T(8,128)}, ...) custom-call(bf16[2,2,2,384,384]{4,3,2,1,0:T(8,128)(2,1)} %bitcast.159, ...), custom_call_target="tpu_custom_call" | custom-call | tf_op jit(solution)/shard_map/reduce_gradients/pallas_call | solution.py:351
  (465 shorter events, 223.9 us)
Async XLA Ops:
  3.5 163.2 %copy-start.62 = (f32[392]{0:T(512)}, f32[392]{0:T(512)S(1)}, u32[]{:S(2)}) copy-start(f32[392]{0:T(512)S(1)} %div.118) | copy-start | bytes 4708
  4.6 161.5 %copy-start.23 = (bf16[1,8,49,768]{3,1,2,0:T(8,128)(2,1)S(1)}, bf16[1,8,49,768]{3,1,2,0:T(8,128)(2,1)}, u32[]{:S(2)}) copy-start(bf16[1,8,49,768]{3,1,2,0:T(8,128)(2,1)} %param.25) | copy-start | bytes 1806340
  188.8 288.6 %collective-permute-start.10 = (bf16[392,768]{1,0:T(8,128)(2,1)}, bf16[392,768]{1,0:T(8,128)(2,1)}, u32[]{:S(2)}, u32[]{:S(2)}) collective-permute-start(bf16[392,768]{1,0:T(8,128)(2,1)} %convert_element_type.372), channel_id=1, source_target_pairs={{0,4},{4,0},{8,12},{12,8},{16,20},{20,16},{24,28},{28,24},{1,5},{5... | collective-permute-start | bytes 1806344 | tf_op jit(solution)/shard_map/ppermute | solution.py:364
  192.3 288.2 %collective-permute-start.8 = (bf16[392,768]{1,0:T(8,128)(2,1)}, bf16[392,768]{1,0:T(8,128)(2,1)}, u32[]{:S(2)}, u32[]{:S(2)}) collective-permute-start(bf16[392,768]{1,0:T(8,128)(2,1)} %fusion.45), channel_id=1, source_target_pairs={{0,4},{4,0},{8,12},{12,8},{16,20},{20,16},{24,28},{28,24},{1,5},{5... | collective-permute-start | bytes 1806344 | tf_op jit(solution)/shard_map/ppermute | solution.py:364
  195.9 23.7 %all-to-all-start = ((bf16[1,8,49,768]{3,2,0,1:T(8,128)(2,1)}), bf16[1,8,49,768]{3,2,0,1:T(8,128)(2,1)}, u32[]{:S(2)}, u32[]{:S(2)}) async-start(bf16[1,8,49,768]{3,2,0,1:T(8,128)(2,1)} %bitcast.8), calls=%async_computation | async-start | bytes 1376256 | tf_op jit(solution)/shard_map/all_to_all | solution.py:620
  280.4 12.3 %copy-start.86 = (bf16[1,768]{1,0:T(2,128)(2,1)S(1)}, bf16[1,768]{1,0:T(2,128)(2,1)}, u32[]{:S(2)}) copy-start(bf16[1,768]{1,0:T(2,128)(2,1)} %param.26) | copy-start | bytes 4612
  294.7 15.6 %slice-start.2 = ((s8[4718592]{0:T(1024)(128)(4,1)}), s8[4194304]{0:T(1024)(128)(4,1)S(1)}, s32[]{:S(2)}) async-start(s8[4718592]{0:T(1024)(128)(4,1)} %bitcast.170), calls=%async_computation.4 | async-start | bytes 8388608
  295.3 15.0 %copy-start.38 = (bf16[393,768]{1,0:T(8,128)(2,1)}, bf16[393,768]{1,0:T(8,128)(2,1)S(1)}, u32[]{:S(2)}) copy-start(bf16[393,768]{1,0:T(8,128)(2,1)S(1)} %add_convert_fusion.1) | copy-start | bytes 1810948
  295.4 14.9 %slice-start.3 = ((s8[4718592]{0:T(1024)(128)(4,1)}), s8[524288]{0:T(1024)(128)(4,1)S(1)}, s32[]{:S(2)}) async-start(s8[4718592]{0:T(1024)(128)(4,1)} %bitcast.170), calls=%async_computation.5 | async-start | bytes 1048576
  377.9 109.0 %collective-permute-start.6 = (bf16[394,768]{1,0:T(8,128)(2,1)}, bf16[394,768]{1,0:T(8,128)(2,1)}, u32[]{:S(2)}, u32[]{:S(2)}) collective-permute-start(bf16[394,768]{1,0:T(8,128)(2,1)} %add_convert_fusion.2), channel_id=1, source_target_pairs={{0,4},{4,0},{8,12},{12,8},{16,20},{20,16},{24,28},{28,24},{1,5},{5... | collective-permute-start | bytes 1815560 | tf_op jit(solution)/shard_map/ppermute | solution.py:364
  400.5 40.5 %all-to-all-start.1 = ((bf16[1,2,196,768]{3,1,0,2:T(2,128)(2,1)}), bf16[1,2,196,768]{3,1,0,2:T(2,128)(2,1)S(1)}, u32[]{:S(2)}, u32[]{:S(2)}) async-start(bf16[1,2,196,768]{3,1,0,2:T(2,128)(2,1)} %fusion.108), calls=%async_computation.1 | async-start | bytes 1204224 | tf_op jit(solution)/shard_map/all_to_all | solution.py:715
  409.0 14.9 %copy-start.59 = (f32[1,768]{1,0:T(1,128)S(1)}, f32[1,768]{1,0:T(1,128)}, u32[]{:S(2)}) copy-start(f32[1,768]{1,0:T(1,128)} %copy-done.58) | copy-start | bytes 9220
  411.4 23.4 %collective-permute-start.4 = (bf16[394,768]{1,0:T(8,128)(2,1)}, bf16[394,768]{1,0:T(8,128)(2,1)}, u32[]{:S(2)}, u32[]{:S(2)}) collective-permute-start(bf16[394,768]{1,0:T(8,128)(2,1)} %copy.255), channel_id=1, source_target_pairs={{0,4},{4,0},{8,12},{12,8},{16,20},{20,16},{24,28},{28,24},{1,5},{5... | collective-permute-start | bytes 1815560 | tf_op jit(solution)/shard_map/ppermute | solution.py:364
  426.4 11.2 %collective-permute-start.5 = (bf16[394,384]{1,0:T(8,128)(2,1)}, bf16[394,384]{1,0:T(8,128)(2,1)}, u32[]{:S(2)}, u32[]{:S(2)}) collective-permute-start(bf16[394,384]{1,0:T(8,128)(2,1)} %get-tuple-element.226), channel_id=1, source_target_pairs={{0,4},{4,0},{8,12},{12,8},{16,20},{20,16},{24,28},{28,24},{1,5},{5... | collective-permute-start | bytes 907784 | tf_op jit(solution)/shard_map/ppermute | solution.py:364
  434.8 76.2 %collective-permute-start = (bf16[393,3072]{1,0:T(8,128)(2,1)}, bf16[393,3072]{1,0:T(8,128)(2,1)}, u32[]{:S(2)}, u32[]{:S(2)}) collective-permute-start(bf16[393,3072]{1,0:T(8,128)(2,1)} %get-tuple-element.207), channel_id=1, source_target_pairs={{0,4},{4,0},{8,12},{12,8},{16,20},{20,16},{24,28},{28,24},{1,5},{5... | collective-permute-start | bytes 7243784 | tf_op jit(solution)/shard_map/ppermute | solution.py:364
  437.6 44.4 %collective-permute-start.7 = (bf16[394,1152]{1,0:T(8,128)(2,1)}, bf16[394,1152]{1,0:T(8,128)(2,1)}, u32[]{:S(2)}, u32[]{:S(2)}) collective-permute-start(bf16[394,1152]{1,0:T(8,128)(2,1)} %copy.257), channel_id=1, source_target_pairs={{0,4},{4,0},{8,12},{12,8},{16,20},{20,16},{24,28},{28,24},{1,5},{5... | collective-permute-start | bytes 2723336 | tf_op jit(solution)/shard_map/ppermute | solution.py:364
  477.4 23.3 %collective-permute-start.3 = (bf16[393,1536]{1,0:T(8,128)(2,1)}, bf16[393,1536]{1,0:T(8,128)(2,1)}, u32[]{:S(2)}, u32[]{:S(2)}) collective-permute-start(bf16[393,1536]{1,0:T(8,128)(2,1)} %get-tuple-element.218), channel_id=1, source_target_pairs={{0,4},{4,0},{8,12},{12,8},{16,20},{20,16},{24,28},{28,24},{1,5},{5... | collective-permute-start | bytes 3621896 | tf_op jit(solution)/shard_map/ppermute | solution.py:364
  480.5 7.0 %collective-permute-start.11 = (bf16[392,384]{1,0:T(8,128)(2,1)}, bf16[392,384]{1,0:T(8,128)(2,1)}, u32[]{:S(2)}, u32[]{:S(2)}) collective-permute-start(bf16[392,384]{1,0:T(8,128)(2,1)} %get-tuple-element.230), channel_id=1, source_target_pairs={{0,4},{4,0},{8,12},{12,8},{16,20},{20,16},{24,28},{28,24},{1,5},{5... | collective-permute-start | bytes 903176 | tf_op jit(solution)/shard_map/ppermute | solution.py:364
  482.1 5.0 collective-permute-start.14
  486.9 13.6 %collective-permute-start.2 = (bf16[393,768]{1,0:T(8,128)(2,1)}, bf16[393,768]{1,0:T(8,128)(2,1)}, u32[]{:S(2)}, u32[]{:S(2)}) collective-permute-start(bf16[393,768]{1,0:T(8,128)(2,1)} %copy-done.38), channel_id=1, source_target_pairs={{0,4},{4,0},{8,12},{12,8},{16,20},{20,16},{24,28},{28,24},{1,5},{5... | collective-permute-start | bytes 1810952 | tf_op jit(solution)/shard_map/ppermute | solution.py:364
  487.1 19.3 %collective-permute-start.13 = (bf16[392,1152]{1,0:T(8,128)(2,1)S(1)}, bf16[392,1152]{1,0:T(8,128)(2,1)}, u32[]{:S(2)}, u32[]{:S(2)}) collective-permute-start(bf16[392,1152]{1,0:T(8,128)(2,1)S(1)} %copy-done.37), channel_id=1, source_target_pairs={{0,4},{4,0},{8,12},{12,8},{16,20},{20,16},{24,28},{28,24},{1,5},{5... | collective-permute-start | bytes 2709512 | tf_op jit(solution)/shard_map/ppermute | solution.py:364
  487.5 6.1 collective-permute-start.9
  493.6 12.8 %collective-permute-start.12 = (bf16[392,768]{1,0:T(8,128)(2,1)}, bf16[392,768]{1,0:T(8,128)(2,1)S(1)}, u32[]{:S(2)}, u32[]{:S(2)}) collective-permute-start(bf16[392,768]{1,0:T(8,128)(2,1)} %copy-done.40), channel_id=1, source_target_pairs={{0,4},{4,0},{8,12},{12,8},{16,20},{20,16},{24,28},{28,24},{1,5},{5... | collective-permute-start | bytes 1806344 | tf_op jit(solution)/shard_map/ppermute | solution.py:364
  500.5 10.5 %collective-permute-start.1 = (bf16[393,384]{1,0:T(8,128)(2,1)S(1)}, bf16[393,384]{1,0:T(8,128)(2,1)S(1)}, u32[]{:S(2)}, u32[]{:S(2)}) collective-permute-start(bf16[393,384]{1,0:T(8,128)(2,1)S(1)} %copy-done.48), channel_id=1, source_target_pairs={{0,4},{4,0},{8,12},{12,8},{16,20},{20,16},{24,28},{28,24},{1,5},{5... | collective-permute-start | bytes 905480 | tf_op jit(solution)/shard_map/ppermute | solution.py:364
  (101 other events, 372.7 us)
